TPU v7x, 32 devices: a whole 2x2x4 slice. The times are simulated.
32 devices in a mesh: ulysses: 4 (over x, core), blk: 8 (over z, y).
Axes of the slice: x: 2, y: 2, z: 4, core: 2. Of those that a mesh axis runs over, the one named last changes fastest.
Arguments:
- inputs: bfloat16 [8, 512, 1024], P('blk', 'ulysses'), may hold values from -6 to 6
- cotangent: bfloat16 [8, 512, 1024], P('blk', 'ulysses'), may hold values from -6 to 6
- segment_ids: int32 [8, 512], replicated, may hold values from 0 to 30, as said below
- bucket_table: int32 [257], replicated, may hold values from 0 to 31, as said below
- gain_attention: float32 [1024], replicated, may hold values from 0.5 to 1.5
- query_weight: bfloat16 [1024, 1024], P(('ulysses', 'blk')), may hold values from -0.046875 to 0.046875
- key_weight: bfloat16 [1024, 1024], P(('ulysses', 'blk')), may hold values from -0.1875 to 0.1875
- value_weight: bfloat16 [1024, 1024], P(('ulysses', 'blk')), may hold values from -0.1875 to 0.1875
- output_weight: bfloat16 [1024, 1024], P(('ulysses', 'blk')), may hold values from -0.75 to 0.75
- bucket_bias: float32 [32, 16], replicated, may hold values from -3 to 3
- gain_feedforward: float32 [1024], replicated, may hold values from 0.5 to 1.5
- gate_weight: bfloat16 [2816, 1024], P(('ulysses', 'blk')), may hold values from -0.1875 to 0.1875
- up_weight: bfloat16 [2816, 1024], P(('ulysses', 'blk')), may hold values from -0.1875 to 0.1875
- down_weight: bfloat16 [2816, 1024], P(('ulysses', 'blk')), may hold values from -0.109375 to 0.109375
Outputs:
- layer_out: bfloat16 [8, 512, 1024], P('blk', 'ulysses')
- grad_inputs: bfloat16 [8, 512, 1024], P('blk', 'ulysses')
- grad_gain_attention: float32 [1024], replicated
- grad_query_weight: float32 [1024, 1024], P(('ulysses', 'blk'))
- grad_key_weight: float32 [1024, 1024], P(('ulysses', 'blk'))
- grad_value_weight: float32 [1024, 1024], P(('ulysses', 'blk'))
- grad_output_weight: float32 [1024, 1024], P(('ulysses', 'blk'))
- grad_bucket_bias: float32 [32, 16], replicated
- grad_gain_feedforward: float32 [1024], replicated
- grad_gate_weight: float32 [2816, 1024], P(('ulysses', 'blk'))
- grad_up_weight: float32 [2816, 1024], P(('ulysses', 'blk'))
- grad_down_weight: float32 [2816, 1024], P(('ulysses', 'blk'))
Inputs may be any that keep to these rules, and one draw needn't show every extreme that they name: bucket_table[128 + o] is the bucket of a key o positions after its query, for o from -128 to 128 (farther keys take the end entries): 0 at o = 0, 1 to 15 for keys before the query, 16 to 31 for keys after it, never falling as |o| grows, 15 and 31 at the two ends. `segment_ids`: never falling along the sequence. Positions 256 * w to 256 * w + 255 form window w; window 0 is block 0, every later window w holds exactly the two non-empty blocks 2 w - 1 and 2 w.
All inputs are finite; a program needn't handle non-finite values.
Results may differ from a plain program's by a relative error of at most 0.025.
Values may be sent and summed in bfloat16 or wider, within the bound.
No kernel may reach another device: no remote copies, remote signals or barrier semaphores. Data moves between devices by JAX's collectives and lax.ppermute only.
A program may use at most 192 MiB of HBM per device.

v0:
```python
import math

import jax
import jax.numpy as jnp
from jax import lax
from jax.sharding import PartitionSpec as P

EPSILON = 1e-06
NEGATIVE = -1e30
HIGHEST = lax.Precision.HIGHEST


def norm_scale(values):
    return lax.rsqrt(jnp.mean(values * values, axis=-1, keepdims=True) + EPSILON)


def norm_back(values, scaling, gain_vec, upstream):
    inner_sum = jnp.mean(values * gain_vec * upstream, axis=-1, keepdims=True)
    return scaling * gain_vec * upstream - values * scaling * scaling * scaling * inner_sum


def project(left_side, weight):
    return jnp.einsum("td,fd->tf", left_side, weight, preferred_element_type=jnp.float32)


def back_project(gradient, weight):
    return jnp.einsum("tf,fd->td", gradient, weight, preferred_element_type=jnp.float32)


def outer_rows(gradient, left_side):
    return jnp.einsum("tf,td->fd", gradient, left_side, preferred_element_type=jnp.float32)


def gated(gate_act, up_act):
    return jax.nn.gelu(gate_act, approximate=True) * up_act


def owner_terms(pair_list, owners, row_count):
    blocks = []
    for columns, left_side in pair_list:
        term_rows = outer_rows(columns, left_side)
        blocks.append(term_rows.reshape(owners, 1, row_count, term_rows.shape[-1]))
    joined = jnp.concatenate(blocks, axis=1)
    return joined.reshape(owners, len(pair_list) * row_count, joined.shape[-1])


def reduce_rows(term_fn, row_count):
    return lax.psum_scatter(
        term_fn(jnp.int32(0), row_count * lax.axis_size("blk")).astype(jnp.bfloat16),
        "blk",
        scatter_dimension=0,
        tiled=True,
    ).astype(jnp.float32)


def in_blocks(step_fn, carried, pieces, limit):
    total_rows = pieces[0].shape[0]
    block_rows = math.gcd(total_rows, limit)
    block_count = total_rows // block_rows

    def one_block(block_at, state):
        offset = block_at * block_rows
        sub_pieces = tuple(
            (lax.dynamic_slice_in_dim(member, offset, block_rows, 0) for member in pieces)
        )
        return step_fn(state, sub_pieces, offset)

    return lax.fori_loop(0, block_count, one_block, carried)


def diagonal_onehot(base, rows, cols, reach_max):
    diag_count = rows + cols
    offsets = base + jnp.arange(diag_count, dtype=jnp.int32) - (rows - 1)
    index_diag = jnp.clip(offsets, -reach_max, reach_max) + reach_max
    return (index_diag[:, None] == jnp.arange(2 * reach_max + 1, dtype=jnp.int32)[None, :]).astype(
        jnp.float32
    )


def spread_diagonals(diag_vals, rows, cols):
    heads_here, diag_count = diag_vals.shape
    tiled = jnp.tile(diag_vals, (1, rows))
    window = tiled[:, rows - 1 : rows - 1 + rows * (diag_count - 1)]
    return window.reshape(heads_here, rows, diag_count - 1)[:, :, :cols]


def collect_diagonals(block_grad, rows, cols):
    heads_here = block_grad.shape[0]
    diag_count = rows + cols
    padded = jnp.pad(block_grad, ((0, 0), (0, 0), (0, diag_count - 1 - cols))).reshape(
        heads_here, rows * (diag_count - 1)
    )
    placed = jnp.concatenate(
        (
            jnp.zeros((heads_here, rows - 1), jnp.float32),
            padded,
            jnp.zeros((heads_here, 1), jnp.float32),
        ),
        axis=1,
    )
    return jnp.sum(placed.reshape(heads_here, rows, diag_count), axis=1)


def body(
    inputs,
    cotangent,
    segment_ids,
    bucket_table,
    gain_attention,
    query_weight,
    key_weight,
    value_weight,
    output_weight,
    bucket_bias,
    gain_feedforward,
    gate_weight,
    up_weight,
    down_weight,
):
    own_tokens = inputs.shape[1]
    model_width = inputs.shape[2]
    ulysses_at = lax.axis_index("ulysses")
    run_at = lax.axis_index("blk")
    gathered_in, gathered_cot = (
        lax.all_gather(inputs, "ulysses", axis=1, tiled=True),
        lax.all_gather(cotangent, "ulysses", axis=1, tiled=True),
    )
    run_tokens = gathered_in.shape[1]
    hidden_in = gathered_in.reshape(run_tokens, model_width).astype(jnp.float32)
    cot_rows = gathered_cot.reshape(run_tokens, model_width)
    query_group, key_group, value_group, output_group = (
        lax.all_gather(query_weight, "blk", axis=0, tiled=True),
        lax.all_gather(key_weight, "blk", axis=0, tiled=True),
        lax.all_gather(value_weight, "blk", axis=0, tiled=True),
        lax.all_gather(output_weight, "blk", axis=0, tiled=True),
    )
    group_width = query_group.shape[0]
    head_count = bucket_bias.shape[1]
    group_heads = head_count // lax.axis_size("ulysses")
    head_dim = group_width // group_heads
    reach_max = (bucket_table.shape[0] - 1) // 2
    bucket_count = bucket_bias.shape[0]
    segment_flat = segment_ids.reshape(-1)
    first_query = run_at * run_tokens
    query_seg = lax.dynamic_slice_in_dim(segment_flat, first_query, run_tokens, 0)
    onehot = (bucket_table[:, None] == jnp.arange(bucket_count, dtype=jnp.int32)[None, :]).astype(
        jnp.float32
    )
    table_all = jnp.dot(onehot, bucket_bias, precision=HIGHEST)
    table_group = lax.dynamic_slice_in_dim(table_all, ulysses_at * group_heads, group_heads, 1)
    first_row = ulysses_at * own_tokens

    def bias_block(diag_table, rows, cols):
        diag_vals = jnp.dot(diag_table, table_group, precision=HIGHEST).T
        return spread_diagonals(diag_vals, rows, cols)

    def head_scores(query_cols, key_cols, bias_head, allowed):
        raw_scores = jnp.einsum(
            "qd,kd->qk", query_cols, key_cols, preferred_element_type=jnp.float32
        )
        return jnp.where(allowed, raw_scores + bias_head, NEGATIVE)

    def head_columns(head_idx):
        return slice(head_idx * head_dim, (head_idx + 1) * head_dim)

    scale_first = norm_scale(hidden_in)
    normed = (hidden_in * scale_first * gain_attention).astype(jnp.bfloat16)
    queries = project(normed, query_group).astype(jnp.bfloat16)
    keys_local = project(normed, key_group).astype(jnp.bfloat16)
    values_local = project(normed, value_group).astype(jnp.bfloat16)

    def forward_block(carried, pieces, piece_start):
        run_peak, totals, accumulated = carried
        key_piece, value_piece = pieces
        piece_rows = key_piece.shape[0]
        key_seg = lax.dynamic_slice_in_dim(segment_flat, piece_start, piece_rows, 0)
        allowed = key_seg[None, :] <= query_seg[:, None]
        diag_table = diagonal_onehot(piece_start - first_query, run_tokens, piece_rows, reach_max)
        biases = bias_block(diag_table, run_tokens, piece_rows)
        head_peaks, row_sums, head_parts = ([], [], [])
        for head_idx in range(group_heads):
            columns = head_columns(head_idx)
            scores = head_scores(
                queries[:, columns], key_piece[:, columns], biases[head_idx], allowed
            )
            new_peak = jnp.maximum(run_peak[head_idx], jnp.max(scores, axis=1))
            weights = jnp.where(allowed, jnp.exp(scores - new_peak[:, None]), 0.0)
            factor = jnp.exp(run_peak[head_idx] - new_peak)
            row_sums.append(totals[head_idx] * factor + jnp.sum(weights, axis=1))
            mixed_part = jnp.dot(
                weights.astype(jnp.bfloat16),
                value_piece[:, columns],
                preferred_element_type=jnp.float32,
            )
            head_parts.append(accumulated[:, columns] * factor[:, None] + mixed_part)
            head_peaks.append(new_peak)
        return (jnp.stack(head_peaks), jnp.stack(row_sums), jnp.concatenate(head_parts, axis=1))

    start_state = (
        jnp.full((group_heads, run_tokens), NEGATIVE, jnp.float32),
        jnp.zeros((group_heads, run_tokens), jnp.float32),
        jnp.zeros((run_tokens, group_width), jnp.float32),
    )
    run_peak, totals, accumulated = in_blocks(
        forward_block,
        start_state,
        (
            lax.all_gather(keys_local, "blk", axis=0, tiled=True),
            lax.all_gather(values_local, "blk", axis=0, tiled=True),
        ),
        run_tokens,
    )
    log_total = run_peak + jnp.log(totals)
    attended = (
        accumulated.reshape(run_tokens, group_heads, head_dim) / totals.T[:, :, None]
    ).reshape(run_tokens, group_width)
    attended_low = attended.astype(jnp.bfloat16)
    branch_part = jnp.dot(attended_low, output_group, preferred_element_type=jnp.float32)
    branch = lax.psum(branch_part.astype(jnp.bfloat16), "ulysses").astype(jnp.float32)
    middle = hidden_in + branch
    scale_second = norm_scale(middle)
    normed_mid = (middle * scale_second * gain_feedforward).astype(jnp.bfloat16)
    middle_own = lax.dynamic_slice_in_dim(middle, first_row, own_tokens, 0)
    gate_piece = lax.all_gather(gate_weight, "blk", axis=0, tiled=True)
    up_piece = lax.all_gather(up_weight, "blk", axis=0, tiled=True)
    down_piece = lax.all_gather(down_weight, "blk", axis=0, tiled=True)
    hidden = gated(project(normed_mid, gate_piece), project(normed_mid, up_piece)).astype(
        jnp.bfloat16
    )
    feed_part = jnp.dot(hidden, down_piece, preferred_element_type=jnp.float32)
    feed_own = lax.psum_scatter(
        feed_part.astype(jnp.bfloat16), "ulysses", scatter_dimension=0, tiled=True
    ).astype(jnp.float32)
    layer_out = (middle_own + feed_own).astype(jnp.bfloat16).reshape(1, own_tokens, model_width)
    gate_piece = lax.all_gather(gate_weight, "blk", axis=0, tiled=True)
    up_piece = lax.all_gather(up_weight, "blk", axis=0, tiled=True)
    down_piece = lax.all_gather(down_weight, "blk", axis=0, tiled=True)
    gate_act = project(normed_mid, gate_piece)
    up_act = project(normed_mid, up_piece)
    hidden_val, pullback = jax.vjp(gated, gate_act, up_act)
    grad_hidden = project(cot_rows, down_piece)
    grad_gate, grad_up = pullback(grad_hidden)
    gate_low = grad_gate.astype(jnp.bfloat16)
    up_low = grad_up.astype(jnp.bfloat16)
    grad_norm = back_project(gate_low, gate_piece) + back_project(up_low, up_piece)
    stacked = jnp.stack((gate_low, up_low, hidden_val.astype(jnp.bfloat16)))
    saved_acts = stacked
    grad_norm_part, saved_acts = (grad_norm, saved_acts)
    grad_norm_mid = lax.psum(grad_norm_part.astype(jnp.bfloat16), "ulysses").astype(jnp.float32)
    grad_middle = cot_rows.astype(jnp.float32) + norm_back(
        middle, scale_second, gain_feedforward, grad_norm_mid
    )
    gain_second_term = jnp.sum(
        lax.dynamic_slice_in_dim(grad_norm_mid * middle * scale_second, first_row, own_tokens, 0),
        axis=0,
    )
    grad_mid_low = grad_middle.astype(jnp.bfloat16)
    grad_middle_own = lax.dynamic_slice_in_dim(grad_middle, first_row, own_tokens, 0)
    feed_rows = gate_weight.shape[0]
    feed_pairs = (
        (saved_acts[0], normed_mid),
        (saved_acts[1], normed_mid),
        (saved_acts[2], cot_rows),
    )

    def feed_terms(piece_start, piece_rows):
        per_owner = 3 * feed_rows
        owners = piece_rows // per_owner
        return owner_terms(feed_pairs, owners, feed_rows).reshape(owners * per_owner, model_width)

    feed_grads = reduce_rows(feed_terms, 3 * feed_rows)
    grad_attended = project(grad_mid_low, output_group)
    grad_att_low = grad_attended.astype(jnp.bfloat16)
    row_delta = jnp.sum(
        (grad_att_low.astype(jnp.float32) * attended).reshape(run_tokens, group_heads, head_dim),
        axis=2,
    ).T
    log_all, delta_all = (
        lax.all_gather(log_total, "blk", axis=1, tiled=True),
        lax.all_gather(row_delta, "blk", axis=1, tiled=True),
    )

    def key_block(carried, pieces, piece_start):
        grad_query, grad_table = carried
        key_piece, value_piece = pieces
        piece_rows = key_piece.shape[0]
        key_seg = lax.dynamic_slice_in_dim(segment_flat, piece_start, piece_rows, 0)
        allowed = key_seg[None, :] <= query_seg[:, None]
        diag_table = diagonal_onehot(piece_start - first_query, run_tokens, piece_rows, reach_max)
        biases = bias_block(diag_table, run_tokens, piece_rows)
        query_parts, score_parts = ([], [])
        for head_idx in range(group_heads):
            columns = head_columns(head_idx)
            scores = head_scores(
                queries[:, columns], key_piece[:, columns], biases[head_idx], allowed
            )
            prob_rows = jnp.where(allowed, jnp.exp(scores - log_total[head_idx][:, None]), 0.0)
            grad_probs = jnp.einsum(
                "qd,kd->qk",
                grad_att_low[:, columns],
                value_piece[:, columns],
                preferred_element_type=jnp.float32,
            )
            grad_scores = (prob_rows * (grad_probs - row_delta[head_idx][:, None])).astype(
                jnp.bfloat16
            )
            query_parts.append(
                jnp.dot(grad_scores, key_piece[:, columns], preferred_element_type=jnp.float32)
            )
            score_parts.append(grad_scores.astype(jnp.float32))
        diag_sums = collect_diagonals(jnp.stack(score_parts), run_tokens, piece_rows)
        table_step = jnp.dot(diag_sums, diag_table, precision=HIGHEST)
        return (grad_query + jnp.concatenate(query_parts, axis=1), grad_table + table_step)

    key_state = (
        jnp.zeros((run_tokens, group_width), jnp.float32),
        jnp.zeros((group_heads, 2 * reach_max + 1), jnp.float32),
    )
    grad_queries, grad_table = in_blocks(
        key_block,
        key_state,
        (
            lax.all_gather(keys_local, "blk", axis=0, tiled=True),
            lax.all_gather(values_local, "blk", axis=0, tiled=True),
        ),
        run_tokens,
    )

    def query_block(carried, pieces, piece_start):
        grad_key, grad_value = carried
        query_piece, grad_piece = pieces
        piece_rows = query_piece.shape[0]
        rows_seg = lax.dynamic_slice_in_dim(segment_flat, piece_start, piece_rows, 0)
        log_piece = lax.dynamic_slice_in_dim(log_all, piece_start, piece_rows, 1)
        delta_piece = lax.dynamic_slice_in_dim(delta_all, piece_start, piece_rows, 1)
        allowed = query_seg[None, :] <= rows_seg[:, None]
        diag_table = diagonal_onehot(first_query - piece_start, piece_rows, run_tokens, reach_max)
        biases = bias_block(diag_table, piece_rows, run_tokens)
        key_parts, value_parts = ([], [])
        for head_idx in range(group_heads):
            columns = head_columns(head_idx)
            scores = head_scores(
                query_piece[:, columns], keys_local[:, columns], biases[head_idx], allowed
            )
            prob_rows = jnp.where(allowed, jnp.exp(scores - log_piece[head_idx][:, None]), 0.0)
            grad_probs = jnp.einsum(
                "qd,kd->qk",
                grad_piece[:, columns],
                values_local[:, columns],
                preferred_element_type=jnp.float32,
            )
            grad_scores = (prob_rows * (grad_probs - delta_piece[head_idx][:, None])).astype(
                jnp.bfloat16
            )
            key_parts.append(
                jnp.einsum(
                    "qk,qd->kd",
                    grad_scores,
                    query_piece[:, columns],
                    preferred_element_type=jnp.float32,
                )
            )
            value_parts.append(
                jnp.einsum(
                    "qk,qd->kd",
                    prob_rows.astype(jnp.bfloat16),
                    grad_piece[:, columns],
                    preferred_element_type=jnp.float32,
                )
            )
        return (
            grad_key + jnp.concatenate(key_parts, axis=1),
            grad_value + jnp.concatenate(value_parts, axis=1),
        )

    query_state = (
        jnp.zeros((run_tokens, group_width), jnp.float32),
        jnp.zeros((run_tokens, group_width), jnp.float32),
    )
    grad_keys, grad_values = in_blocks(
        query_block,
        query_state,
        (
            lax.all_gather(queries, "blk", axis=0, tiled=True),
            lax.all_gather(grad_att_low, "blk", axis=0, tiled=True),
        ),
        run_tokens,
    )
    query_low = grad_queries.astype(jnp.bfloat16)
    key_low = grad_keys.astype(jnp.bfloat16)
    value_low = grad_values.astype(jnp.bfloat16)
    grad_normed = (
        back_project(query_low, query_group)
        + back_project(key_low, key_group)
        + back_project(value_low, value_group)
    )
    grad_part = norm_back(hidden_in, scale_first, gain_attention, grad_normed)
    gain_first_term = jnp.sum(grad_normed * hidden_in * scale_first, axis=0)
    grad_own = lax.psum_scatter(
        grad_part.astype(jnp.bfloat16), "ulysses", scatter_dimension=0, tiled=True
    ).astype(jnp.float32)
    grad_inputs = (
        (grad_middle_own + grad_own).astype(jnp.bfloat16).reshape(1, own_tokens, model_width)
    )
    table_full = jnp.zeros((2 * reach_max + 1, head_count), jnp.float32)
    table_full = lax.dynamic_update_slice_in_dim(
        table_full, grad_table.T, ulysses_at * group_heads, 1
    )
    bias_term = jnp.dot(onehot.T, table_full, precision=HIGHEST)
    gain_first_grad, gain_second_grad, bias_grad = lax.psum(
        (gain_first_term, gain_second_term, bias_term), ("ulysses", "blk")
    )
    attention_rows = query_weight.shape[0]
    attention_pairs = (
        (query_low, normed),
        (key_low, normed),
        (value_low, normed),
        (attended_low, grad_mid_low),
    )

    def attention_terms(piece_start, piece_rows):
        per_owner = 4 * attention_rows
        owners = piece_rows // per_owner
        return owner_terms(attention_pairs, owners, attention_rows).reshape(
            owners * per_owner, model_width
        )

    attention_grads = reduce_rows(attention_terms, 4 * attention_rows)
    attention_grads = attention_grads.reshape(4, attention_rows, model_width)
    feed_grads = feed_grads.reshape(3, feed_rows, model_width)
    return (
        layer_out,
        grad_inputs,
        gain_first_grad,
        attention_grads[0],
        attention_grads[1],
        attention_grads[2],
        attention_grads[3],
        bias_grad,
        gain_second_grad,
        feed_grads[0],
        feed_grads[1],
        feed_grads[2],
    )


def solution(mesh):
    return jax.shard_map(
        body,
        mesh=mesh,
        in_specs=(
            P("blk", "ulysses", None),
            P("blk", "ulysses", None),
            P(),
            P(),
            P(),
            P(("ulysses", "blk"), None),
            P(("ulysses", "blk"), None),
            P(("ulysses", "blk"), None),
            P(("ulysses", "blk"), None),
            P(),
            P(),
            P(("ulysses", "blk"), None),
            P(("ulysses", "blk"), None),
            P(("ulysses", "blk"), None),
        ),
        out_specs=(
            P("blk", "ulysses", None),
            P("blk", "ulysses", None),
            P(),
            P(("ulysses", "blk"), None),
            P(("ulysses", "blk"), None),
            P(("ulysses", "blk"), None),
            P(("ulysses", "blk"), None),
            P(),
            P(),
            P(("ulysses", "blk"), None),
            P(("ulysses", "blk"), None),
            P(("ulysses", "blk"), None),
        ),
        check_vma=False,
    )
```

profile of v0, /device:TPU:0, one launch (start us, length us, event | category | flops | bytes accessed | tf_op | source)
XLA Modules:
  0.0 3048.6 jit_solution(2191271173832576940)
XLA Ops:
  8.0 33.2 %all_gather.51 = bf16[256,1024]{1,0:T(8,128)(2,1)S(1)} all-gather(bf16[32,1024]{1,0:T(8,128)(2,1)} %param.26), channel_id=1, replica_groups=mesh['ulysses'=4,'blk'=8] {'blk'}, dimensions={0}, use_global_device_ids=true | all-gather | bytes 589824 | tf_op jit(solution)/shard_map/all_gather | solution.py:133
  45.6 32.0 %all_gather.54 = bf16[256,1024]{1,0:T(8,128)(2,1)S(1)} all-gather(bf16[32,1024]{1,0:T(8,128)(2,1)S(1)} %copy-done.58), channel_id=1, replica_groups=mesh['ulysses'=4,'blk'=8] {'blk'}, dimensions={0}, use_global_device_ids=true | all-gather | bytes 589824 | tf_op jit(solution)/shard_map/all_gather | solution.py:134
  82.0 32.3 %all_gather.53 = bf16[256,1024]{1,0:T(8,128)(2,1)S(1)} all-gather(bf16[32,1024]{1,0:T(8,128)(2,1)S(1)} %copy-done.59), channel_id=1, replica_groups=mesh['ulysses'=4,'blk'=8] {'blk'}, dimensions={0}, use_global_device_ids=true | all-gather | bytes 589824 | tf_op jit(solution)/shard_map/all_gather | solution.py:132
  114.3 32.5 %all_gather.56 = bf16[256,1024]{1,0:T(8,128)(2,1)S(1)} all-gather(bf16[32,1024]{1,0:T(8,128)(2,1)S(1)} %copy-done.60), channel_id=1, replica_groups=mesh['ulysses'=4,'blk'=8] {'blk'}, dimensions={0}, use_global_device_ids=true | all-gather | bytes 589824 | tf_op jit(solution)/shard_map/all_gather | solution.py:135
  157.4 582.2 %while.55 = (s32[]{:T(128)}, f32[4,512]{1,0:T(4,128)S(1)}, f32[4,512]{1,0:T(4,128)}, f32[512,256]{0,1:T(8,128)S(1)}, s32[4096]{0:T(1024)}, /*index=5*/s32[512]{0...) while((s32[]{:T(128)}, f32[4,512]{1,0:T(4,128)S(1)}, ...), condition=%wide.region_10.11_spmd, body=%wide.region_1.10_spmd.sunk | while | flops 293807104 | bytes 105206448 | solution.py:68
  186.2 15.8 reshape.519
  622.5 15.8 reshape.519
  695.2 15.8 reshape.519
  744.7 33.2 %all-reduce.5.cloned.1.call-done = bf16[512,1024]{1,0:T(8,128)(2,1)} async-done(((bf16[512,1024]{1,0:T(8,128)(2,1)}), bf16[512,1024]{1,0:T(8,128)(2,1)}) %all-reduce.5.cloned.1.call-update) | async-done | bytes 1048592 | tf_op jit(solution)/shard_map/psum | solution.py:219
  781.1 42.6 %all-gather.16.cloned.1.call-done = bf16[704,1024]{1,0:T(8,128)(2,1)} async-done(((bf16[88,1024]{1,0:T(8,128)(2,1)}), bf16[704,1024]{1,0:T(8,128)(2,1)}) %all-gather.16.cloned.1.call-update) | async-done | bytes 1441808 | tf_op jit(solution)/shard_map/all_gather | solution.py:224
  827.3 40.0 %all-gather.18.cloned.1.call-done = bf16[704,1024]{1,0:T(8,128)(2,1)} async-done(((bf16[88,1024]{1,0:T(8,128)(2,1)}), bf16[704,1024]{1,0:T(8,128)(2,1)}) %all-gather.18.cloned.1.call-update) | async-done | bytes 1441808 | tf_op jit(solution)/shard_map/all_gather | solution.py:225
  884.0 45.5 %all-gather.20.cloned.1.call-done = bf16[704,1024]{1,0:T(8,128)(2,1)} async-done(((bf16[88,1024]{1,0:T(8,128)(2,1)}), bf16[704,1024]{1,0:T(8,128)(2,1)}) %all-gather.20.cloned.1.call-update) | async-done | bytes 1441808 | tf_op jit(solution)/shard_map/all_gather | solution.py:226
  938.7 33.9 %all-reduce.7.cloned.1.call-done = bf16[512,1024]{1,0:T(8,128)(2,1)} async-done(((bf16[512,1024]{1,0:T(8,128)(2,1)}), bf16[512,1024]{1,0:T(8,128)(2,1)}) %all-reduce.7.cloned.1.call-update) | async-done | bytes 1048592 | tf_op jit(solution)/shard_map/psum | solution.py:249
  979.6 32.8 %all_gather.62 = f32[4,4096]{1,0:T(4,128)} all-gather(f32[4,512]{1,0:T(4,128)S(1)} %log_add_fusion), channel_id=1, replica_groups=mesh['ulysses'=4,'blk'=8] {'blk'}, dimensions={1}, use_global_device_ids=true | all-gather | bytes 73728 | tf_op jit(solution)/shard_map/all_gather | solution.py:279
  1016.6 32.5 %all_gather.64 = f32[4,4096]{1,0:T(4,128)} all-gather(f32[4,512]{1,0:T(4,128)S(1)} %bitcast.489), channel_id=1, replica_groups=mesh['ulysses'=4,'blk'=8] {'blk'}, dimensions={1}, use_global_device_ids=true | all-gather | bytes 73728 | tf_op jit(solution)/shard_map/all_gather | solution.py:280
  1049.1 1255.9 %while.56 = (s32[]{:T(128)}, f32[512,256]{0,1:T(8,128)}, f32[4,257]{1,0:T(4,128)}, s32[4096]{0:T(1024)}, s32[512]{0:T(512)S(1)}, /*index=5*/bf16[4096,256]{1,0:T...) while((s32[]{:T(128)}, f32[512,256]{0,1:T(8,128)}, ...), condition=%wide.region_19.20_spmd.clone, body=%wide.region_17.19_spmd.clone.sunk | while | flops 466823168 | bytes 170685296 | solution.py:68
  1101.8 15.8 reshape.521
  1170.3 43.7 %dynamic-update-slice.7 = f32[4,524288]{1,0:T(4,128)} dynamic-update-slice(f32[4,524288]{1,0:T(4,128)} %dynamic-update-slice.6, f32[4,523776]{1,0:T(4,128)} %reshape.522, s32[]{} %constant.579..sunk, s32[]{} %constant.580..sunk) | dynamic-update-slice | bytes 16760836 | tf_op jit(solution)/shard_map/while
  1253.2 15.8 reshape.521
  1322.8 43.7 %dynamic-update-slice.7 = f32[4,524288]{1,0:T(4,128)} dynamic-update-slice(f32[4,524288]{1,0:T(4,128)} %dynamic-update-slice.6, f32[4,523776]{1,0:T(4,128)} %reshape.522, s32[]{} %constant.579..sunk, s32[]{} %constant.580..sunk) | dynamic-update-slice | bytes 16760836 | tf_op jit(solution)/shard_map/while
  1475.2 43.7 %dynamic-update-slice.7 = f32[4,524288]{1,0:T(4,128)} dynamic-update-slice(f32[4,524288]{1,0:T(4,128)} %dynamic-update-slice.6, f32[4,523776]{1,0:T(4,128)} %reshape.522, s32[]{} %constant.579..sunk, s32[]{} %constant.580..sunk) | dynamic-update-slice | bytes 16760836 | tf_op jit(solution)/shard_map/while
  1627.5 43.7 %dynamic-update-slice.7 = f32[4,524288]{1,0:T(4,128)} dynamic-update-slice(f32[4,524288]{1,0:T(4,128)} %dynamic-update-slice.6, f32[4,523776]{1,0:T(4,128)} %reshape.522, s32[]{} %constant.579..sunk, s32[]{} %constant.580..sunk) | dynamic-update-slice | bytes 16760836 | tf_op jit(solution)/shard_map/while
  1779.9 43.7 %dynamic-update-slice.7 = f32[4,524288]{1,0:T(4,128)} dynamic-update-slice(f32[4,524288]{1,0:T(4,128)} %dynamic-update-slice.6, f32[4,523776]{1,0:T(4,128)} %reshape.522, s32[]{} %constant.579..sunk, s32[]{} %constant.580..sunk) | dynamic-update-slice | bytes 16760836 | tf_op jit(solution)/shard_map/while
  1862.8 15.8 reshape.521
  1932.4 43.7 %dynamic-update-slice.7 = f32[4,524288]{1,0:T(4,128)} dynamic-update-slice(f32[4,524288]{1,0:T(4,128)} %dynamic-update-slice.6, f32[4,523776]{1,0:T(4,128)} %reshape.522, s32[]{} %constant.579..sunk, s32[]{} %constant.580..sunk) | dynamic-update-slice | bytes 16760836 | tf_op jit(solution)/shard_map/while
  2084.8 43.7 %dynamic-update-slice.7 = f32[4,524288]{1,0:T(4,128)} dynamic-update-slice(f32[4,524288]{1,0:T(4,128)} %dynamic-update-slice.6, f32[4,523776]{1,0:T(4,128)} %reshape.522, s32[]{} %constant.579..sunk, s32[]{} %constant.580..sunk) | dynamic-update-slice | bytes 16760836 | tf_op jit(solution)/shard_map/while
  2167.6 15.8 reshape.521
  2237.1 43.7 %dynamic-update-slice.7 = f32[4,524288]{1,0:T(4,128)} dynamic-update-slice(f32[4,524288]{1,0:T(4,128)} %dynamic-update-slice.6, f32[4,523776]{1,0:T(4,128)} %reshape.522, s32[]{} %constant.579..sunk, s32[]{} %constant.580..sunk) | dynamic-update-slice | bytes 16760836 | tf_op jit(solution)/shard_map/while
  2309.8 535.7 %while.57 = (s32[]{:T(128)}, f32[512,256]{0,1:T(8,128)S(1)}, f32[512,256]{0,1:T(8,128)S(1)}, s32[512]{0:T(512)S(1)}, s32[4096]{0:T(1024)}, /*index=5*/bf16[4096,...) while((s32[]{:T(128)}, f32[512,256]{0,1:T(8,128)S(1)}, ...), condition=%wide.region_21.22_spmd.clone, body=%wide.region_20.21_spmd.clone.sunk | while | flops 560518144 | bytes 85032568 | solution.py:68
  2869.4 39.7 %all-reduce.1 = (f32[1024]{0:T(1024)}, f32[32,16]{0,1:T(8,128)}, f32[1024]{0:T(1024)}) all-reduce(f32[1024]{0:T(1024)S(1)} %get-tuple-element.1044, f32[32,16]{0,1:T(8,128)S(1)} %fusion.241, f32[1024]{0:T(1024)S(1)} %get-tuple-element.1193), channel_id=1, replica_groups=mesh['ulysses'=4,'blk'=8] {'ulysses','blk'}, use_global_device_ids=true, to_apply=%region_25.26 | all-reduce | flops 2560 | bytes 20480 | tf_op jit(solution)/shard_map/psum | solution.py:410
  2910.8 36.5 %reduce-scatter.9.cloned.1.call-done = bf16[128,1024]{1,0:T(8,128)(2,1)} async-done(((bf16[1024,1024]{1,0:T(8,128)(2,1)}), bf16[128,1024]{1,0:T(8,128)(2,1)}) %reduce-scatter.9.cloned.1.call-update) | async-done | bytes 262160 | tf_op jit(solution)/shard_map/reduce_scatter | solution.py:48
  2949.1 90.7 %reduce-scatter.11.cloned.1.call-done = bf16[264,1024]{1,0:T(8,128)(2,1)} async-done(((bf16[2112,1024]{1,0:T(8,128)(2,1)}), bf16[264,1024]{1,0:T(8,128)(2,1)}) %reduce-scatter.11.cloned.1.call-update) | async-done | bytes 540688 | tf_op jit(solution)/shard_map/reduce_scatter | solution.py:48
  (1320 shorter events, 1973.7 us)
Async XLA Ops:
  7.2 73.9 %copy-start = (f32[32,16]{0,1:T(8,128)S(1)}, f32[32,16]{0,1:T(8,128)}, u32[]{:S(2)}) copy-start(f32[32,16]{0,1:T(8,128)} %param.29) | copy-start | bytes 6148
  7.2 34.0 %all-gather.10.cloned.1.call-start = ((), (), s32[]{:S(2)}) async-start(), calls=%async_computation.4 | async-start | bytes 1310720 | tf_op jit(solution)/shard_map/all_gather | solution.py:125
  7.9 139.4 %all-gather.12.cloned.1.call-start = ((), (), s32[]{:S(2)}) async-start(), calls=%async_computation.5 | async-start | bytes 2359296 | tf_op jit(solution)/shard_map/all_gather | solution.py:208
  43.0 103.8 %copy-start.63 = (f32[512]{0:T(512)}, f32[512]{0:T(512)S(1)}, u32[]{:S(2)}) copy-start(f32[512]{0:T(512)S(1)} %add_rsqrt_fusion.1) | copy-start | bytes 6148
  45.5 36.5 %copy-start.59 = (bf16[32,1024]{1,0:T(8,128)(2,1)S(1)}, bf16[32,1024]{1,0:T(8,128)(2,1)}, u32[]{:S(2)}) copy-start(bf16[32,1024]{1,0:T(8,128)(2,1)} %param.25) | copy-start | bytes 196612
  45.5 111.2 %all-gather.14.cloned.1.call-start = ((), (), s32[]{:S(2)}) async-start(), calls=%async_computation.6 | async-start | bytes 2359296 | tf_op jit(solution)/shard_map/all_gather | solution.py:209
  79.7 698.2 %all-reduce.5.cloned.1.call-start = ((), (), s32[]{:S(2)}) async-start(), calls=%async_computation.7 | async-start | bytes 2097152 | tf_op jit(solution)/shard_map/psum | solution.py:219
  114.3 42.4 %copy-start.33 = (bf16[256,1024]{1,0:T(8,128)(2,1)}, bf16[256,1024]{1,0:T(8,128)(2,1)S(1)}, u32[]{:S(2)}) copy-start(bf16[256,1024]{1,0:T(8,128)(2,1)S(1)} %all_gather.53) | copy-start | bytes 1572868
  739.6 38.3 %copy-start.8 = (bf16[1,512,1024]{2,1,0:T(8,128)(2,1)S(1)}, bf16[1,512,1024]{2,1,0:T(8,128)(2,1)}, u32[]{:S(2)}) copy-start(bf16[1,512,1024]{2,1,0:T(8,128)(2,1)} %all-gather.10.cloned.1.call-done) | copy-start | bytes 3145732
  742.0 37.7 %copy-start.62 = (f32[1024]{0:T(1024)S(1)}, f32[1024]{0:T(1024)}, u32[]{:S(2)}) copy-start(f32[1024]{0:T(1024)} %param.30) | copy-start | bytes 12292
  742.0 81.6 %all-gather.16.cloned.1.call-start = ((), (), s32[]{:S(2)}) async-start(), calls=%async_computation.8 | async-start | bytes 1622016 | tf_op jit(solution)/shard_map/all_gather | solution.py:224
  742.6 124.7 %all-gather.18.cloned.1.call-start = ((), (), s32[]{:S(2)}) async-start(), calls=%async_computation.9 | async-start | bytes 1622016 | tf_op jit(solution)/shard_map/all_gather | solution.py:225
  743.1 140.9 %all-gather.22.cloned.1.call-start = ((), (), s32[]{:S(2)}) async-start(), calls=%async_computation.12 | async-start | bytes 1310720 | tf_op jit(solution)/shard_map/all_gather | solution.py:126
  743.9 185.6 %all-gather.20.cloned.1.call-start = ((), (), s32[]{:S(2)}) async-start(), calls=%async_computation.10 | async-start | bytes 1622016 | tf_op jit(solution)/shard_map/all_gather | solution.py:226
  744.7 228.0 %all-reduce.7.cloned.1.call-start = ((), (), s32[]{:S(2)}) async-start(), calls=%async_computation.13 | async-start | bytes 2097152 | tf_op jit(solution)/shard_map/psum | solution.py:249
  779.7 194.9 %copy-start.65 = (f32[512]{0:T(512)}, f32[512]{0:T(512)S(1)}, u32[]{:S(2)}) copy-start(f32[512]{0:T(512)S(1)} %add_rsqrt_fusion) | copy-start | bytes 6148
  938.1 1371.7 %all-gather.24.cloned.1.call-start = ((), (), s32[]{:S(2)}) async-start(), calls=%async_computation.14 | async-start | bytes 2359296 | tf_op jit(solution)/shard_map/all_gather | solution.py:384
  938.6 1371.2 %all-gather.26.cloned.1.call-start = ((), (), s32[]{:S(2)}) async-start(), calls=%async_computation.15 | async-start | bytes 2359296 | tf_op jit(solution)/shard_map/all_gather | solution.py:385
  979.5 1887.9 %reduce-scatter.5.cloned.1.call-start = ((), (), s32[]{:S(2)}) async-start(), calls=%async_computation.11 | async-start | bytes 1310720 | tf_op jit(solution)/shard_map/reduce_scatter | solution.py:231
  1012.4 36.8 %copy-start.3 = (bf16[512,256]{1,0:T(8,128)(2,1)S(1)}, bf16[512,256]{1,0:T(8,128)(2,1)}, u32[]{:S(2)}) copy-start(bf16[512,256]{1,0:T(8,128)(2,1)} %copy-done.2) | copy-start | bytes 786436
  1016.4 1892.7 %reduce-scatter.7.cloned.1.call-start = ((), (), s32[]{:S(2)}) async-start(), calls=%async_computation.16 | async-start | bytes 1310720 | tf_op jit(solution)/shard_map/reduce_scatter | solution.py:399
  2310.6 55.6 %copy-start.61 = (s32[512]{0:T(512)}, s32[512]{0:T(512)S(1)}, u32[]{:S(2)}) copy-start(s32[512]{0:T(512)S(1)} %dynamic_slice.158) | copy-start | bytes 6148 | tf_op jit(solution)/shard_map/while
  2377.6 55.6 %copy-start.61 = (s32[512]{0:T(512)}, s32[512]{0:T(512)S(1)}, u32[]{:S(2)}) copy-start(s32[512]{0:T(512)S(1)} %dynamic_slice.158) | copy-start | bytes 6148 | tf_op jit(solution)/shard_map/while
  2444.5 55.6 %copy-start.61 = (s32[512]{0:T(512)}, s32[512]{0:T(512)S(1)}, u32[]{:S(2)}) copy-start(s32[512]{0:T(512)S(1)} %dynamic_slice.158) | copy-start | bytes 6148 | tf_op jit(solution)/shard_map/while
  2511.4 55.6 %copy-start.61 = (s32[512]{0:T(512)}, s32[512]{0:T(512)S(1)}, u32[]{:S(2)}) copy-start(s32[512]{0:T(512)S(1)} %dynamic_slice.158) | copy-start | bytes 6148 | tf_op jit(solution)/shard_map/while
  2578.4 55.6 %copy-start.61 = (s32[512]{0:T(512)}, s32[512]{0:T(512)S(1)}, u32[]{:S(2)}) copy-start(s32[512]{0:T(512)S(1)} %dynamic_slice.158) | copy-start | bytes 6148 | tf_op jit(solution)/shard_map/while
  2645.3 55.6 %copy-start.61 = (s32[512]{0:T(512)}, s32[512]{0:T(512)S(1)}, u32[]{:S(2)}) copy-start(s32[512]{0:T(512)S(1)} %dynamic_slice.158) | copy-start | bytes 6148 | tf_op jit(solution)/shard_map/while
  2712.3 55.6 %copy-start.61 = (s32[512]{0:T(512)}, s32[512]{0:T(512)S(1)}, u32[]{:S(2)}) copy-start(s32[512]{0:T(512)S(1)} %dynamic_slice.158) | copy-start | bytes 6148 | tf_op jit(solution)/shard_map/while
  2779.2 55.6 %copy-start.61 = (s32[512]{0:T(512)}, s32[512]{0:T(512)S(1)}, u32[]{:S(2)}) copy-start(s32[512]{0:T(512)S(1)} %dynamic_slice.158) | copy-start | bytes 6148 | tf_op jit(solution)/shard_map/while
  2850.6 96.7 %reduce-scatter.9.cloned.1.call-start = ((), (), s32[]{:S(2)}) async-start(), calls=%async_computation.17 | async-start | bytes 2359296 | tf_op jit(solution)/shard_map/reduce_scatter | solution.py:48
  2855.8 184.0 %reduce-scatter.11.cloned.1.call-start = ((), (), s32[]{:S(2)}) async-start(), calls=%async_computation.18 | async-start | bytes 4866048 | tf_op jit(solution)/shard_map/reduce_scatter | solution.py:48
  2869.4 172.4 %copy-start.1 = (f32[32,16]{0,1:T(8,128)S(1)}, f32[32,16]{0,1:T(8,128)}, u32[]{:S(2)}) copy-start(f32[32,16]{0,1:T(8,128)} %param.29) | copy-start | bytes 6148
  (253 other events, 1097.6 us)
Sparse Core Ops, SparseCore 0:
  9.6 19.4 all-gather.9
  45.7 58.7 all-gather.11
  107.1 49.5 all-gather.13
  742.1 35.7 all-reduce.4
  780.1 43.4 all-gather.15
  825.9 41.3 all-gather.17
  868.9 15.0 all-gather.21
  886.4 43.0 all-gather.19
  938.2 34.3 all-reduce.6
  975.2 50.2 all-gather.23
  1028.1 49.4 all-gather.25
  1079.9 23.0 reduce-scatter.4
  2850.8 24.9 reduce-scatter.6
  2879.1 68.1 reduce-scatter.8
  2950.8 88.9 reduce-scatter.10
where the time goes:
time: 3080 us; the launch traced here: 3050 us
  local copies, waits for them, and re-layouts  1790 us (58%)
  matrix products  473 us (15%)
  waiting for transfers between devices  348 us (11%)
  blocking collectives  235 us (8%)
  other arithmetic  147 us (5%)
  loops' own time  42.6 us (1%)
    while x560, local copies, waits for them, and re-layouts  868 us
    reshape x24, local copies, waits for them, and re-layouts, spread_diagonals(): return window.reshape(heads_here, rows, diag_count - 1)[:, :, :cols]  379 us
    slice x24, local copies, waits for them, and re-layouts, spread_diagonals(): window = tiled[:, rows - 1:rows - 1 + rows * (diag_count - 1)]  222 us
    reshape x16, local copies, waits for them, and re-layouts, collect_diagonals(): jnp.pad(block_grad, ((0, 0), (0, 0), (0, diag_count - 1 - cols)))  190 us
    dot_general x96, matrix products, head_scores(): jnp.einsum('qd,kd->qk', query_cols, key_cols, preferred_element_type=jnp....  158 us
    reduce_scatter x2, waiting for transfers between devices, reduce_rows(): lax.psum_scatter(term_fn(jnp.int32(0), row_count * lax.axis_size('blk'))....  127 us
    reduce_sum x8, other arithmetic, collect_diagonals(): return jnp.sum(placed.reshape(heads_here, rows, diag_count), axis=1)  62.3 us
  transfers between devices with their start and end apart: 15, of which 9 were waited for; matrix products, arithmetic and copies ran while one was open for 59% of the time, Pallas kernels for 0%

commit v1 on v0

v1 whole, which is shorter than its diff:
```python
import functools

import jax
import jax.numpy as jnp
from jax import lax
from jax.experimental import pallas as pl
from jax.experimental.pallas import tpu as pltpu
from jax.sharding import Mesh
from jax.sharding import PartitionSpec as P

EPSILON = 1e-06
NEGATIVE = -1e30
HIGHEST = lax.Precision.HIGHEST
F32 = jnp.float32
BF16 = jnp.bfloat16
VMEM_LIMIT = 60 * 1024 * 1024
SQUARE = ("x", "y")
HEADS_GROUP = ("x", "c", "y", "r")
UNITS_GROUP = ("c", "z", "r")
EVERY = ("x", "c", "z", "y", "r")


def norm_scale(values):
    return lax.rsqrt(jnp.mean(values * values, axis=-1, keepdims=True) + EPSILON)


def norm_back(values, scaling, gain_vec, upstream):
    inner_sum = jnp.mean(values * gain_vec * upstream, axis=-1, keepdims=True)
    return scaling * gain_vec * upstream - values * scaling * scaling * scaling * inner_sum


def nt(left, right):
    return lax.dot_general(left, right, (((1,), (1,)), ((), ())), preferred_element_type=F32)


def nn(left, right):
    return lax.dot_general(left, right, (((1,), (0,)), ((), ())), preferred_element_type=F32)


def tn(left, right):
    return lax.dot_general(left, right, (((0,), (0,)), ((), ())), preferred_element_type=F32)


def swap(value, axis, mask):
    size = lax.axis_size(axis)
    return lax.ppermute(value, axis, [(at, at ^ mask) for at in range(size)])


def from_group(value, axis):
    return [value] + [swap(value, axis, mask) for mask in (1, 2, 3)]


def to_group(values, axis):
    return [values[0]] + [swap(values[mask], axis, mask) for mask in (1, 2, 3)]


def kernel_call(body, out_shapes, inputs, scratch=(), scalars=1):
    in_specs = [pl.BlockSpec(memory_space=pltpu.SMEM)] * scalars
    in_specs += [pl.BlockSpec(memory_space=pltpu.VMEM)] * (len(inputs) - scalars)
    return pl.pallas_call(
        body,
        out_shape=out_shapes,
        in_specs=in_specs,
        out_specs=jax.tree.map(lambda _: pl.BlockSpec(memory_space=pltpu.VMEM), out_shapes),
        scratch_shapes=list(scratch),
        compiler_params=pltpu.CompilerParams(vmem_limit_bytes=VMEM_LIMIT),
    )(*inputs)


def shape(dims, dtype):
    return jax.ShapeDtypeStruct(dims, dtype)


def qkv_body(hd, coords, *refs):
    blocks, (wa, wb), pieces = refs[:4], refs[4:6], refs[6:10]
    rows_all, weights = refs[10:12]
    x_at, c_at, y_at = coords[0], coords[1], coords[3]
    tokens, width = blocks[0].shape
    for at in range(4):
        rows_all[at * tokens : (at + 1) * tokens, :] = blocks[at][...]
    for dest in range(4):
        base = pl.multiple_of((x_at ^ (dest >> 1)) * hd, hd)
        other = (y_at ^ (dest & 1)) ^ c_at

        def put(source, base=base, dest=dest):
            for kind, start in ((0, 8 * hd + dest * hd), (1, dest * 2 * hd), (2, dest * 2 * hd + hd)):
                weights[start : start + hd, :] = source[
                    pl.ds(base, hd), kind * width : (kind + 1) * width
                ]

        pl.when(other == 0)(functools.partial(put, wa))
        pl.when(other == 1)(functools.partial(put, wb))
    normed = rows_all[...]
    pairs = nt(normed, weights[0 : 8 * hd, :]).astype(BF16)
    queries = nt(weights[8 * hd : 12 * hd, :], normed).astype(BF16)
    for dest in range(4):
        pieces[dest][0 : 4 * tokens, :] = pairs[:, dest * 2 * hd : (dest + 1) * 2 * hd]
        for at in range(4):
            pieces[dest][4 * tokens + at * hd : 4 * tokens + (at + 1) * hd, :] = queries[
                dest * hd : (dest + 1) * hd, at * tokens : (at + 1) * tokens
            ]


def bias_tiles(hvec, tokens):
    tiles = {}
    for at, diff in enumerate((-1, 0, 1)):
        spread = jnp.broadcast_to(hvec[at : at + 1, :], (tokens, 2 * tokens))
        tiles[diff] = pltpu.roll(spread, 0, 1, stride=1, stride_axis=0)[:, :tokens]
    return tiles


def fill_bias(hvec_ref, bias, c_at, tokens):
    tiles = bias_tiles(hvec_ref[...], tokens)
    zero = jnp.zeros((tokens, tokens), F32)
    for rows in range(8):
        for half in range(2):
            diff = rows - 4 - 2 * half
            even, odd = tiles.get(diff, zero), tiles.get(diff - 1, zero)
            bias[rows * tokens : (rows + 1) * tokens, half * tokens : (half + 1) * tokens] = (
                jnp.where(c_at == 0, even, odd)
            )


def allowed_mask(cuts, run, c_at, tokens):
    rows, cols = 4 * tokens, 2 * tokens
    key_at = lax.broadcasted_iota(jnp.int32, (rows, cols), 0)
    query_at = lax.broadcasted_iota(jnp.int32, (rows, cols), 1)
    key_window = key_at >= 2 * tokens
    query_window = query_at >= tokens
    key_in = jnp.where(key_window, key_at - 2 * tokens, key_at)
    query_in = jnp.where(query_window, query_at - tokens, query_at) + c_at * tokens
    cut = jnp.where(query_window, cuts[2 * run + 1], cuts[2 * run])
    inside = (key_in < cut) | (query_in >= cut)
    before = jnp.logical_and(jnp.logical_not(key_window), query_window)
    same = key_window == query_window
    return before | (same & inside)


def fold_rows(values, how):
    rows, cols = values.shape
    return how(values.reshape(rows // 8, 8, cols), axis=0)


def attend_body(tokens, hd, repeat, coords, cuts, hvec, *refs):
    pieces, own, other = refs[:4], refs[4:8], refs[8:12]
    if repeat == 1:
        pieces = refs[:4]
        own, other, refs = refs[:4], refs[4:8], refs[8:]
    else:
        refs = refs[12:]
    out, out_near, lse, attended, keys, keys_t, queries, scores, bias = refs
    x_at, c_at, z_at, y_at, r_at = (coords[at] for at in range(5))
    block = 4 * tokens
    for dest in range(4):
        x_from, y_from = x_at ^ (dest >> 1), y_at ^ (dest & 1)
        for at in range(4):
            place = (z_at ^ at) * 2 + y_from
            for rep in range(repeat):
                run = place * repeat + rep
                base = run * block + x_from * 2 * tokens
                source = slice(rep * block + at * tokens, rep * block + (at + 1) * tokens)
                keys[pl.ds(pl.multiple_of(base + c_at * tokens, tokens), tokens), :] = own[dest][
                    source, :
                ]
                keys[pl.ds(pl.multiple_of(base + (1 - c_at) * tokens, tokens), tokens), :] = other[
                    dest
                ][source, :]
            start = block + at * hd
            queries[place, :, pl.ds(pl.multiple_of(x_from * tokens, tokens), tokens)] = pieces[
                dest
            ][start : start + hd, :]
    fill_bias(hvec, bias, c_at, tokens)

    def turn(at, carry):
        rows = pl.ds(pl.multiple_of(at * block, block), block)
        keys_t[at] = keys[rows, :].T
        return carry

    lax.fori_loop(0, keys.shape[0] // block, turn, 0)

    def one_block(place, carry):
        run = place * repeat + r_at
        query_t = queries[place]
        query_pad = jnp.concatenate([query_t, jnp.zeros_like(query_t)], axis=0)

        def raw(at):
            return nn(keys[pl.ds(pl.multiple_of(at * block, block), block), :], query_pad)

        def far(at, peak):
            values = raw(at)
            scores[at] = values
            return jnp.maximum(peak, fold_rows(values, jnp.max))

        def near(at, peak):
            values = raw(at) + bias[0:block, :]
            scores[at] = values
            return jnp.maximum(peak, fold_rows(values, jnp.max))

        last = raw(run) + bias[block:, :]
        last = jnp.where(allowed_mask(cuts, run, c_at, tokens), last, NEGATIVE)
        scores[run] = last
        peak = fold_rows(last, jnp.max)
        peak = lax.fori_loop(jnp.maximum(run - 1, 0), run, near, peak)
        peak = lax.fori_loop(0, run - 1, far, peak)
        top = jnp.max(peak, axis=0, keepdims=True)

        def mix(at, state):
            total, mixed = state
            weights = jnp.exp(scores[at] - top)
            total = total + fold_rows(weights, jnp.sum)
            mixed = mixed + nn(keys_t[at, hd:, :], weights.astype(BF16))
            return total, mixed

        start = (jnp.zeros((8, 2 * tokens), F32), jnp.zeros((hd, 2 * tokens), F32))
        total, mixed = lax.fori_loop(0, run + 1, mix, start)
        total = jnp.sum(total, axis=0, keepdims=True)
        mixed = mixed / total
        attended[place] = mixed
        lse[place] = jnp.broadcast_to(top + jnp.log(total), (8, 2 * tokens))
        low = mixed.astype(BF16)
        z_to, y_to = place >> 1, place & 1
        for half in range(2):
            part = low[:, half * tokens : (half + 1) * tokens]
            out[half * 8 + y_to * 4 + z_to] = part
            out_near[((x_at ^ half) * 2 + (y_to ^ y_at)) * 4 + (z_to ^ z_at)] = part
        return carry

    lax.fori_loop(0, queries.shape[0], one_block, 0)


def attend_back_body(tokens, hd, repeat, coords, cuts, hvec, *refs):
    arrived, queries, keys, keys_t, attended, lse = refs[:6]
    grad_own, grad_other, grad_q, table_out, far_out = refs[6:11]
    bias, grad_keys, table_acc = refs[11:]
    x_at, c_at, z_at, y_at, r_at = (coords[at] for at in range(5))
    block = 4 * tokens
    fill_bias(hvec, bias, c_at, tokens)
    grad_keys[...] = jnp.zeros_like(grad_keys)
    table_acc[...] = jnp.zeros_like(table_acc)
    far_out[...] = jnp.zeros_like(far_out)

    def one_block(place, carry):
        run = place * repeat + r_at
        z_to, y_to = place >> 1, place & 1
        query_t = queries[place]
        upstream_t = jnp.concatenate(
            [arrived[half * 8 + y_to * 4 + z_to] for half in range(2)], axis=1
        )
        zero = jnp.zeros_like(query_t)
        query_pad = jnp.concatenate([query_t, zero], axis=0)
        upstream_pad = jnp.concatenate([zero, upstream_t], axis=0)
        query_rows = query_pad.T
        upstream_rows = upstream_pad.T
        shift = lse[place][0:1, :]
        delta = jnp.sum(upstream_t.astype(F32) * attended[place], axis=0, keepdims=True)

        def finish(at, values, mask=None):
            rows = pl.ds(pl.multiple_of(at * block, block), block)
            probs = jnp.exp(values - shift)
            if mask is not None:
                probs = jnp.where(mask, probs, 0.0)
            grad_probs = nn(keys[rows, :], upstream_pad)
            grad_scores = probs * (grad_probs - delta)
            grad_low = grad_scores.astype(BF16)
            grad_keys[rows, :] += nn(grad_low, query_rows) + nn(probs.astype(BF16), upstream_rows)
            return grad_low, nn(keys_t[at, :hd, :], grad_low)

        def raw(at):
            return nn(keys[pl.ds(pl.multiple_of(at * block, block), block), :], query_pad)

        def far(at, grad_query):
            grad_low, step = finish(at, raw(at))
            far_out[...] += fold_rows(grad_low.astype(F32), jnp.sum)
            return grad_query + step

        def near(at, grad_query):
            grad_low, step = finish(at, raw(at) + bias[0:block, :])
            table_acc[0:block, :] += grad_low.astype(F32)
            return grad_query + step

        grad_low, grad_query = finish(
            run, raw(run) + bias[block:, :], allowed_mask(cuts, run, c_at, tokens)
        )
        table_acc[block:, :] += grad_low.astype(F32)
        grad_query = lax.fori_loop(jnp.maximum(run - 1, 0), run, near, grad_query)
        grad_query = lax.fori_loop(0, run - 1, far, grad_query)
        low = grad_query.astype(BF16)
        for half in range(2):
            part = low[:, half * tokens : (half + 1) * tokens]
            grad_q[((x_at ^ half) * 2 + (y_to ^ y_at)) * 4 + (z_to ^ z_at)] = part
        return carry

    lax.fori_loop(0, queries.shape[0], one_block, 0)

    for dest in range(4):
        x_from, y_from = x_at ^ (dest >> 1), y_at ^ (dest & 1)
        for at in range(4):
            place = (z_at ^ at) * 2 + y_from
            for rep in range(repeat):
                base = (place * repeat + rep) * block + x_from * 2 * tokens
                start = (dest * repeat + rep) * block + at * tokens
                target = slice(start, start + tokens)
                grad_own[target, :] = grad_keys[
                    pl.ds(pl.multiple_of(base + c_at * tokens, tokens), tokens), :
                ]
                grad_other[target, :] = grad_keys[
                    pl.ds(pl.multiple_of(base + (1 - c_at) * tokens, tokens), tokens), :
                ].astype(BF16)

    def tile_at(rows, half):
        return table_acc[
            rows * tokens : (rows + 1) * tokens, half * tokens : (half + 1) * tokens
        ]

    spots = [(rows, half) for rows in range(8) for half in range(2)]
    flip = (
        lax.broadcasted_iota(jnp.int32, (tokens, tokens), 0)
        + lax.broadcasted_iota(jnp.int32, (tokens, tokens), 1)
        == tokens - 1
    ).astype(F32)
    far_even = jnp.zeros((tokens, tokens), F32)
    far_odd = jnp.zeros((tokens, tokens), F32)
    for rows, half in spots:
        diff = rows - 4 - 2 * half
        if diff <= -2:
            far_even += tile_at(rows, half)
        if diff - 1 <= -2:
            far_odd += tile_at(rows, half)
    extra = fold_rows(jnp.where(c_at == 0, far_even, far_odd), jnp.sum)
    far_out[:, :tokens] += extra
    table_out[...] = jnp.zeros_like(table_out)
    for index, diff in enumerate((-1, 0, 1)):
        even = sum(tile_at(rows, half) for rows, half in spots if rows - 4 - 2 * half == diff)
        odd = sum(tile_at(rows, half) for rows, half in spots if rows - 5 - 2 * half == diff)
        tile = jnp.where(c_at == 0, even, odd)
        turned = jnp.dot(flip, tile, precision=HIGHEST, preferred_element_type=F32)
        wide = jnp.concatenate([turned, jnp.zeros_like(turned)], axis=1)
        wide = pltpu.roll(wide, tokens + 1, 1, stride=1, stride_axis=0)
        table_out[index : index + 1, :] = jnp.sum(wide, axis=0, keepdims=True)


def project_back_body(hd, coords, *refs):
    pieces, (rows_all, weights, gain), outs = refs[:4], refs[4:7], refs[7:11]
    weight_out, gain_out = refs[11:13]
    pairs, pairs_t, queries, queries_t = refs[13:]
    x_at, c_at, y_at = coords[0], coords[1], coords[3]
    tokens, width = outs[0].shape
    for dest in range(4):
        lanes = slice(dest * 2 * hd, (dest + 1) * 2 * hd)
        part = pieces[dest][0 : 4 * tokens, :]
        pairs[:, lanes] = part
        pairs_t[lanes, :] = part.T
        for at in range(4):
            queries_t[dest * hd : (dest + 1) * hd, at * tokens : (at + 1) * tokens] = pieces[dest][
                4 * tokens + at * hd : 4 * tokens + (at + 1) * hd, :
            ]
    queries[...] = queries_t[...].T
    normed = rows_all[...]
    grad = nn(pairs[...], weights[0 : 8 * hd, :]) + nn(queries[...], weights[8 * hd :, :])
    unit = normed.astype(F32) / gain[...]
    gain_out[...] = fold_rows(grad * unit, jnp.sum)
    for at in range(4):
        outs[at][...] = grad[at * tokens : (at + 1) * tokens, :].astype(BF16)
    pair_rows = nn(pairs_t[...], normed).astype(BF16)
    query_rows = nn(queries_t[...], normed).astype(BF16)
    for dest in range(4):
        head = (x_at ^ (dest >> 1)) * 2 + (y_at ^ (dest & 1))
        rows = pl.ds(pl.multiple_of(head * hd, hd), hd)
        weight_out[rows, 0:width] = query_rows[dest * hd : (dest + 1) * hd, :]
        start = dest * 2 * hd
        weight_out[rows, width : 2 * width] = pair_rows[start : start + hd, :]
        weight_out[rows, 2 * width : 3 * width] = pair_rows[start + hd : start + 2 * hd, :]


def output_back_body(hd, coords, *refs):
    pieces, blocks, weight_out, rows_all, features = refs[:4], refs[4:8], refs[8], refs[9], refs[10]
    x_at, y_at = coords[0], coords[3]
    tokens = blocks[0].shape[0]
    for at in range(4):
        rows_all[at * tokens : (at + 1) * tokens, :] = blocks[at][...]
    for dest in range(4):
        for at in range(4):
            features[dest * hd : (dest + 1) * hd, at * tokens : (at + 1) * tokens] = pieces[dest][at]
    result = nn(features[...], rows_all[...]).astype(BF16)
    for dest in range(4):
        head = (x_at ^ (dest >> 1)) * 2 + (y_at ^ (dest & 1))
        weight_out[pl.ds(pl.multiple_of(head * hd, hd), hd), :] = result[
            dest * hd : (dest + 1) * hd, :
        ]


def gated(gate_act, up_act):
    return jax.nn.gelu(gate_act, approximate=True) * up_act


def body(
    inputs,
    cotangent,
    segment_ids,
    bucket_table,
    gain_attention,
    query_weight,
    key_weight,
    value_weight,
    output_weight,
    bucket_bias,
    gain_feedforward,
    gate_weight,
    up_weight,
    down_weight,
):
    tokens, width = inputs.shape[1:]
    repeat = lax.axis_size("r")
    x_at, c_at, z_at, y_at, r_at = (lax.axis_index(name) for name in EVERY)
    coords = jnp.stack([x_at, c_at, z_at, y_at, r_at]).astype(jnp.int32)
    bucket_count, head_count = bucket_bias.shape
    hd = width // head_count
    block = 4 * tokens
    length = segment_ids.size
    reach = (bucket_table.shape[0] - 1) // 2
    assert reach == tokens and lax.axis_size("x") == lax.axis_size("c") == 2

    hidden_in = inputs[0].astype(F32)
    cot_own = cotangent[0]
    scale_first = norm_scale(hidden_in)
    normed = (hidden_in * scale_first * gain_attention).astype(BF16)
    normed_parts = from_group(normed, "z")

    joined = jnp.concatenate([query_weight, key_weight, value_weight, output_weight], axis=1)
    head_rows = lax.all_gather(joined, ("x", "y", "r"), axis=0, tiled=True)
    head_rows_other = swap(head_rows, "c", 1)
    out_z = lax.all_gather(head_rows[:, 3 * width :], "z", axis=0, tiled=False)
    out_z_other = swap(out_z, "c", 1)
    out_first = jnp.where(c_at == 0, out_z, out_z_other).reshape(4, 2, hd, width)
    out_second = jnp.where(c_at == 0, out_z_other, out_z).reshape(4, 2, hd, width)
    out_full = jnp.stack([out_first, out_second]).transpose(2, 0, 1, 3, 4).reshape(width, width)
    units = jnp.concatenate([gate_weight, up_weight, down_weight], axis=1)
    unit_rows = lax.all_gather(units, UNITS_GROUP, axis=0, tiled=True)
    gate_piece, up_piece, down_piece = (
        unit_rows[:, at * width : (at + 1) * width] for at in range(3)
    )
    cot_all = jnp.concatenate(from_group(cot_own, SQUARE), axis=0)

    windows = segment_ids.reshape(-1, 2 * tokens)
    cuts = jnp.sum((windows < windows[:, -1:]).astype(jnp.int32), axis=1)
    turned = bucket_table[::-1]
    low_half, high_half = turned[reach : 2 * reach], turned[:reach]
    spots = jnp.concatenate(
        [
            jnp.broadcast_to(bucket_table[:1], (reach,)),
            low_half,
            low_half,
            high_half,
            high_half,
            jnp.broadcast_to(bucket_table[2 * reach :], (reach,)),
        ]
    )
    buckets = jnp.arange(bucket_count, dtype=jnp.int32)
    onehot = (spots[:, None] == buckets[None, :]).astype(F32)
    far_onehot = (bucket_table[0] == buckets).astype(F32)
    head_at = (x_at * 2 + y_at) * 4 + z_at
    bias_col = lax.dynamic_slice_in_dim(bucket_bias, head_at, 1, 1)[:, 0]
    diag = jnp.dot(onehot, bias_col, precision=HIGHEST) - jnp.sum(far_onehot * bias_col)
    hvec = jnp.pad(diag.reshape(3, 2 * reach), ((0, 5), (0, 0)))

    made = kernel_call(
        functools.partial(qkv_body, hd),
        [shape((block + 4 * hd, 2 * hd), BF16)] * 4
        + [shape((block, width), BF16), shape((12 * hd, width), BF16)],
        [coords, *normed_parts, head_rows[:, : 3 * width], head_rows_other[:, : 3 * width]],
    )
    pieces, (normed_all, group_weights) = made[:4], made[4:]
    pieces = to_group(pieces, SQUARE)
    own = [piece[:block] for piece in pieces]
    other = swap(jnp.concatenate(own, axis=0), "c", 1)
    other = [other[at * block : (at + 1) * block] for at in range(4)]
    if repeat == 1:
        arrays = [*pieces, *other]
    else:
        own = [lax.all_gather(part, "r", axis=0, tiled=True) for part in own]
        other = [lax.all_gather(part, "r", axis=0, tiled=True) for part in other]
        arrays = [*pieces, *own, *other]
    places = 8
    out_t, out_near, lse, attended, keys, keys_t, queries = kernel_call(
        functools.partial(attend_body, tokens, hd, repeat),
        [
            shape((16, hd, tokens), BF16),
            shape((16, hd, tokens), BF16),
            shape((places, 8, 2 * tokens), F32),
            shape((places, hd, 2 * tokens), F32),
            shape((length, 2 * hd), BF16),
            shape((length // block, 2 * hd, block), BF16),
            shape((places, hd, 2 * tokens), BF16),
        ],
        [coords, cuts, hvec, *arrays],
        [
            pltpu.VMEM((length // block, block, 2 * tokens), F32),
            pltpu.VMEM((2 * block, 2 * tokens), F32),
        ],
        scalars=2,
    )
    arrived = lax.all_to_all(out_t, ("x", "y", "z"), split_axis=0, concat_axis=0, tiled=True)
    near = to_group(
        [out_near[4 * at : 4 * at + 4].reshape(4 * hd, tokens) for at in range(4)], SQUARE
    )

    middle = hidden_in + tn(arrived.reshape(width, tokens), out_full)
    scale_second = norm_scale(middle)
    normed_mid = (middle * scale_second * gain_feedforward).astype(BF16)
    mid_all = jnp.concatenate(from_group(normed_mid, SQUARE), axis=0)

    gate_act = nt(mid_all, gate_piece)
    up_act = nt(mid_all, up_piece)
    hidden_val, pullback = jax.vjp(gated, gate_act, up_act)
    hidden = hidden_val.astype(BF16)
    grad_gate, grad_up = pullback(nt(cot_all, down_piece))
    gate_low, up_low = grad_gate.astype(BF16), grad_up.astype(BF16)
    grad_norm = (nn(gate_low, gate_piece) + nn(up_low, up_piece)).astype(BF16)
    grad_parts = to_group(
        [grad_norm[at * tokens : (at + 1) * tokens] for at in range(4)], SQUARE
    )
    grad_norm_mid = sum(part.astype(F32) for part in grad_parts)
    feed = nn(hidden, down_piece).astype(BF16)
    feed_parts = to_group([feed[at * tokens : (at + 1) * tokens] for at in range(4)], SQUARE)
    layer_out = (middle + sum(part.astype(F32) for part in feed_parts)).astype(BF16)

    grad_middle = cot_own.astype(F32) + norm_back(
        middle, scale_second, gain_feedforward, grad_norm_mid
    )
    gain_second_term = jnp.sum(grad_norm_mid * middle * scale_second, axis=0)
    grad_mid_low = grad_middle.astype(BF16)
    grad_attended = nt(out_full, grad_mid_low).astype(BF16)
    grad_arrived = lax.all_to_all(
        grad_attended.reshape(16, hd, tokens),
        ("x", "y", "z"),
        split_axis=0,
        concat_axis=0,
        tiled=True,
    )
    unit_grads = jnp.concatenate(
        [tn(gate_low, mid_all), tn(up_low, mid_all), tn(hidden, cot_all)], axis=1
    ).astype(BF16)
    unit_grads = lax.psum_scatter(unit_grads, UNITS_GROUP, scatter_dimension=0, tiled=True)

    grad_own, grad_other, grad_q, table_out, far_out = kernel_call(
        functools.partial(attend_back_body, tokens, hd, repeat),
        [
            shape((4 * repeat * block, 2 * hd), F32),
            shape((4 * repeat * block, 2 * hd), BF16),
            shape((16, hd, tokens), BF16),
            shape((8, 2 * tokens), F32),
            shape((8, 2 * tokens), F32),
        ],
        [coords, cuts, hvec, grad_arrived, queries, keys, keys_t, attended, lse],
        [
            pltpu.VMEM((2 * block, 2 * tokens), F32),
            pltpu.VMEM((length, 2 * hd), F32),
            pltpu.VMEM((2 * block, 2 * tokens), F32),
        ],
        scalars=2,
    )
    grad_pairs = (grad_own + swap(grad_other, "c", 1).astype(F32)).astype(BF16)
    grad_pairs = [
        grad_pairs[at * repeat * block : (at + 1) * repeat * block] for at in range(4)
    ]
    if repeat > 1:
        grad_pairs = [
            lax.psum_scatter(part, "r", scatter_dimension=0, tiled=True) for part in grad_pairs
        ]
    grad_pieces = [
        jnp.concatenate([grad_pairs[at], grad_q[4 * at : 4 * at + 4].reshape(4 * hd, tokens)])
        for at in range(4)
    ]
    grad_pieces = to_group(grad_pieces, SQUARE)

    made = kernel_call(
        functools.partial(project_back_body, hd),
        [shape((tokens, width), BF16)] * 4
        + [shape((4 * hd, 3 * width), BF16), shape((8, width), F32)],
        [coords, *grad_pieces, normed_all, group_weights, gain_attention.reshape(1, width)],
        [
            pltpu.VMEM((block, 8 * hd), BF16),
            pltpu.VMEM((8 * hd, block), BF16),
            pltpu.VMEM((block, 4 * hd), BF16),
            pltpu.VMEM((4 * hd, block), BF16),
        ],
    )
    normed_grads, head_grads, gain_first_rows = made[:4], made[4], made[5]
    grad_normed = sum(part.astype(F32) for part in to_group(normed_grads, "z"))
    grad_inputs = (
        grad_middle + norm_back(hidden_in, scale_first, gain_attention, grad_normed)
    ).astype(BF16)

    mid_parts = from_group(grad_mid_low, "z")
    out_grads = kernel_call(
        functools.partial(output_back_body, hd),
        shape((4 * hd, width), BF16),
        [coords, *[part.reshape(4, hd, tokens) for part in near], *mid_parts],
        [pltpu.VMEM((block, width), BF16), pltpu.VMEM((4 * hd, block), BF16)],
    )
    out_grads = lax.psum_scatter(out_grads, HEADS_GROUP, scatter_dimension=0, tiled=True)
    head_grads = lax.psum_scatter(head_grads, HEADS_GROUP, scatter_dimension=0, tiled=True)

    bucket_grad = jnp.dot(table_out[:3].reshape(1, -1), onehot, precision=HIGHEST)[0]
    bucket_grad = bucket_grad + far_onehot * jnp.sum(far_out)
    head_mark = (jnp.arange(head_count) == head_at).astype(F32)
    bias_term = bucket_grad[:, None] * head_mark[None, :]
    gain_first_grad, gain_second_grad, bias_grad = lax.psum(
        (jnp.sum(gain_first_rows, axis=0), gain_second_term, bias_term), EVERY
    )
    head_grads = head_grads.astype(F32)
    unit_grads = unit_grads.astype(F32)
    return (
        layer_out[None],
        grad_inputs[None],
        gain_first_grad,
        head_grads[:, :width],
        head_grads[:, width : 2 * width],
        head_grads[:, 2 * width :],
        out_grads.astype(F32),
        bias_grad,
        gain_second_grad,
        unit_grads[:, :width],
        unit_grads[:, width : 2 * width],
        unit_grads[:, 2 * width :],
    )


def solution(mesh):
    owners, runs = mesh.shape["ulysses"], mesh.shape["blk"]
    fine = Mesh(mesh.devices.reshape(2, owners // 2, 4, 2, runs // 8), EVERY)
    tokens = P(("z", "y", "r"), ("x", "c"), None)
    rows = P(EVERY, None)
    return jax.shard_map(
        body,
        mesh=fine,
        in_specs=(tokens, tokens) + (P(),) * 3 + (rows,) * 4 + (P(),) * 2 + (rows,) * 3,
        out_specs=(tokens, tokens, P()) + (rows,) * 4 + (P(),) * 2 + (rows,) * 3,
        check_vma=False,
    )
```

time: 3080 us -> 436 us (0.14); the launches traced: 3050 us -> 435 us
  local copies, waits for them, and re-layouts: 1790 us -> 18.2 us
  matrix products: 473 us -> 21.2 us
  blocking collectives: 235 us -> 38.7 us
  other arithmetic: 147 us -> 16.7 us
  waiting for transfers between devices: 348 us -> 222 us
  Pallas kernels: 0 us -> 52.5 us
  starting transfers between devices: 0.6 us -> 51.3 us
  loops' own time: 42.6 us -> 0 us
    while x560 -> x0, local copies, waits for them, and re-layouts: 868 us -> none
    reshape x40 -> x2, local copies, waits for them, and re-layouts: 569 us -> 0.01 us  [the longest x1 0.01 us: body(): hvec = jnp.pad(diag.reshape(3, 2 * reach), ((0, 5), (0, 0)))]
    dot_general x311 -> x13, matrix products: 473 us -> 21.2 us  [the longest x4 9.12 us: nt(): lax.dot_general(left, right, (((1,), (1,)), ((), ())), preferred_element_...]
    slice x74 -> x20, local copies, waits for them, and re-layouts: 308 us -> 10.8 us  [the longest x1 2.1 us: body(): unit_grads[:, 2 * width:]]
    all_gather x6 -> x0, blocking collectives: 195 us -> none  [the longest x1 33.2 us: body(): lax.all_gather(key_weight, 'blk', axis=0, tiled=True)]
    all_gather x9 -> x3, waiting for transfers between devices: 150 us -> 33.6 us  [the longest x1 30.8 us: body(): head_rows = lax.all_gather(joined, ('x', 'y', 'r'), axis=0, tiled=True)]
    ppermute x0 -> x34, waiting for transfers between devices: none -> 78.4 us  [swap(): return lax.ppermute(value, axis, [(at, at ^ mask) for at in range(size)])]
    reduce_sum x17 -> x5, other arithmetic: 70.6 us -> 3.43 us  [the longest x1 1.84 us: body(): jnp.sum(far_onehot * bias_col)]
  transfers between devices with their start and end apart: 15 -> 42, of which waited for: 9 -> 26; matrix products, arithmetic and copies ran while one was open for 59% -> 9% of each run, Pallas kernels for 0% -> 12%
where the time goes in v1:
time: 436 us; the launch traced here: 435 us
  waiting for transfers between devices  222 us (51%)
  Pallas kernels  52.5 us (12%)
  starting transfers between devices  51.3 us (12%)
  blocking collectives  38.7 us (9%)
  matrix products  21.2 us (5%)
  local copies, waits for them, and re-layouts  18.2 us (4%)
  other arithmetic  16.7 us (4%)
  between operations  14.9 us (3%)
    reduce_scatter x1, waiting for transfers between devices, body(): lax.psum_scatter(unit_grads, UNITS_GROUP, scatter_dimension=0, tiled=True)  91.9 us
    ppermute x34, waiting for transfers between devices, swap(): return lax.ppermute(value, axis, [(at, at ^ mask) for at in range(size)])  78.4 us
    pallas_call x5, Pallas kernels, kernel_call(): pl.pallas_call(body, out_shape=out_shapes, in_specs=in_specs, out_specs=j...  52.5 us
    psum x1, blocking collectives, body(): lax.psum((jnp.sum(gain_first_rows, axis=0), gain_second_term, bias_term),...  38.7 us
    ppermute x34, starting transfers between devices, swap(): return lax.ppermute(value, axis, [(at, at ^ mask) for at in range(size)])  33.1 us
    all_gather x1, waiting for transfers between devices, body(): head_rows = lax.all_gather(joined, ('x', 'y', 'r'), axis=0, tiled=True)  30.8 us
    all_to_all x1, starting transfers between devices, body(): lax.all_to_all(out_t, ('x', 'y', 'z'), split_axis=0, concat_axis=0, tiled...  13.9 us
    all_to_all x1, waiting for transfers between devices, body(): lax.all_to_all(out_t, ('x', 'y', 'z'), split_axis=0, concat_axis=0, tiled...  10.7 us
  transfers between devices with their start and end apart: 42, of which 26 were waited for; matrix products, arithmetic and copies ran while one was open for 9% of the time, Pallas kernels for 12%

profile of v1, /device:TPU:0, one launch (start us, length us, event | category | flops | bytes accessed | tf_op | source)
XLA Modules:
  0.0 435.5 jit_solution(14938535511625210111)
XLA Ops:
  9.0 30.8 %all-gather.5.cloned.1.call-done = bf16[128,4096]{1,0:T(8,128)(2,1)} async-done(((bf16[32,4096]{1,0:T(8,128)(2,1)}), bf16[128,4096]{1,0:T(8,128)(2,1)}) %all-gather.5.cloned.1.call-update) | async-done | bytes 1048592 | tf_op jit(solution)/shard_map/all_gather | solution.py:430
  45.6 2.4 collective-permute-start.1
  52.4 11.1 %collective-permute-done.refs_1_ = bf16[128,1024]{1,0:T(8,128)(2,1)S(1)} collective-permute-done((bf16[128,1024]{1,0:T(8,128)(2,1)S(1)}, bf16[128,1024]{1,0:T(8,128)(2,1)S(1)}, u32[]{:S(2)}, u32[]{:S(2)}) %collective-permute-start) | collective-permute-done | bytes 262176 | tf_op jit(solution)/shard_map/ppermute | solution.py:46
  63.5 4.3 collective-permute-done.1.refs_2_
  67.8 10.0 %collective-permute-done.2.refs_3_ = bf16[128,1024]{1,0:T(8,128)(2,1)S(1)} collective-permute-done((bf16[128,1024]{1,0:T(8,128)(2,1)S(1)}, bf16[128,1024]{1,0:T(8,128)(2,1)S(1)}, u32[]{:S(2)}, u32[]{:S(2)}) %collective-permute-start.2) | collective-permute-done | bytes 262176 | tf_op jit(solution)/shard_map/ppermute | solution.py:46
  78.5 4.2 shard_map.229
  86.2 2.8 all-gather.9.cloned.1.call-done
  99.7 19.7 %shard_map.230 = (bf16[16,64,128]{2,1,0:T(8,128)(2,1)}, bf16[16,64,128]{2,1,0:T(8,128)(2,1)}, f32[8,8,256]{2,1,0:T(8,128)}, f32[8,64,256]{2,1,0:T(8,128)}, bf16[...) custom-call(s32[5]{0:T(128)} %stack.23.coords, s32[16]{0:T(128)} %convert_reduce_fusion.cuts, ...), custom_call_target="tpu_custom_call" | custom-call | tf_op jit(solution)/shard_map/pallas_call | solution.py:60
  119.4 13.9 %all-to-all-start = ((bf16[16,64,128]{2,1,0:T(8,128)(2,1)}), bf16[16,64,128]{2,1,0:T(8,128)(2,1)S(1)}, u32[]{:S(2)}, u32[]{:S(2)}) async-start(bf16[16,64,128]{2,1,0:T(8,128)(2,1)} %get-tuple-element.40), calls=%async_computation | async-start | bytes 524288 | tf_op jit(solution)/shard_map/all_to_all | solution.py:502
  133.9 10.7 %all-to-all-done = bf16[16,64,128]{2,1,0:T(8,128)(2,1)S(1)} async-done(((bf16[16,64,128]{2,1,0:T(8,128)(2,1)}), bf16[16,64,128]{2,1,0:T(8,128)(2,1)S(1)}, u32[]{:S(2)}, u32[]{:S(2)}) %all-to-all-start) | async-done | bytes 262176 | tf_op jit(solution)/shard_map/all_to_all | solution.py:502
  146.4 2.4 collective-permute-start.9
  150.3 5.2 %collective-permute-done.11 = bf16[128,1024]{1,0:T(8,128)(2,1)S(1)} collective-permute-done((bf16[128,1024]{1,0:T(8,128)(2,1)S(1)}, bf16[128,1024]{1,0:T(8,128)(2,1)S(1)}, u32[]{:S(2)}, u32[]{:S(2)}) %collective-permute-start.11) | collective-permute-done | bytes 262176 | tf_op jit(solution)/shard_map/ppermute | solution.py:46
  155.5 3.8 collective-permute-done.10
  161.3 2.7 fusion.15
  170.2 3.1 multiply_convert_fusion
  182.3 3.4 collective-permute-done.20
  186.3 4.2 collective-permute-done.19
  191.6 5.3 %collective-permute-done.14 = bf16[128,1024]{1,0:T(8,128)(2,1)S(1)} collective-permute-done((bf16[128,1024]{1,0:T(8,128)(2,1)S(1)}, bf16[128,1024]{1,0:T(8,128)(2,1)S(1)}, u32[]{:S(2)}, u32[]{:S(2)}) %collective-permute-start.14) | collective-permute-done | bytes 262176 | tf_op jit(solution)/shard_map/ppermute | solution.py:46
  196.9 2.7 collective-permute-done.13
  204.4 3.8 all-to-all-start.1
  213.0 7.2 %all-to-all-done.1.refs_0_ = bf16[16,64,128]{2,1,0:T(8,128)(2,1)S(1)} async-done(((bf16[16,64,128]{2,1,0:T(8,128)(2,1)}), bf16[16,64,128]{2,1,0:T(8,128)(2,1)S(1)}, u32[]{:S(2)}, u32[]{:S(2)}) %all-to-all-start.1) | async-done | bytes 262176 | tf_op jit(solution)/shard_map/all_to_all | solution.py:533
  220.9 20.8 %shard_map.231 = (f32[2048,128]{1,0:T(8,128)}, bf16[2048,128]{1,0:T(8,128)(2,1)}, bf16[16,64,128]{2,1,0:T(8,128)(2,1)}, f32[8,256]{1,0:T(8,128)}, f32[8,256]{1,0:T(8,128)}) custom-call(s32[5]{0:T(128)} %stack.23.coords, s32[16]{0:T(128)} %convert_reduce_fusion.cuts, f32[8,256]{1,0:T(8,128)} %pad.4.hvec, bf16[16,64,128]{2,1,0:T(8,128)(2,1)} %copy-done.4, ...), custom_call_target="tpu_custom_call" | custom-call | tf_op jit(solution)/shard_map/pallas_call | solution.py:60
  242.4 4.5 %collective-permute-done.28 = bf16[256,128]{1,0:T(8,128)(2,1)S(1)} collective-permute-done((bf16[256,128]{1,0:T(8,128)(2,1)S(1)}, bf16[256,128]{1,0:T(8,128)(2,1)S(1)}, u32[]{:S(2)}, u32[]{:S(2)}) %collective-permute-start.28) | collective-permute-done | bytes 65568 | tf_op jit(solution)/shard_map/ppermute | solution.py:46
  247.4 3.8 collective-permute-done.29
  251.7 4.6 %collective-permute-done.30 = bf16[256,128]{1,0:T(8,128)(2,1)S(1)} collective-permute-done((bf16[256,128]{1,0:T(8,128)(2,1)S(1)}, bf16[256,128]{1,0:T(8,128)(2,1)S(1)}, u32[]{:S(2)}, u32[]{:S(2)}) %collective-permute-start.30) | collective-permute-done | bytes 65568 | tf_op jit(solution)/shard_map/ppermute | solution.py:46
  257.1 2.6 shard_map.233
  261.2 2.5 collective-permute-start.24
  264.4 3.2 collective-permute-done.22.refs_1_
  270.4 5.2 %shard_map.232 = (bf16[128,1024]{1,0:T(8,128)(2,1)}, bf16[128,1024]{1,0:T(8,128)(2,1)}, bf16[128,1024]{1,0:T(8,128)(2,1)}, bf16[128,1024]{1,0:T(8,128)(2,1)}, bf...) custom-call(s32[5]{0:T(128)} %stack.23.coords, bf16[768,128]{1,0:T(8,128)(2,1)} %pad_maximum_fusion.6.refs_0_, ...), custom_call_target="tpu_custom_call" | custom-call | tf_op jit(solution)/shard_map/pallas_call | solution.py:60
  287.0 2.8 collective-permute-start.25
  292.9 38.7 %all-reduce.1 = (f32[1024]{0:T(1024)}, f32[32,16]{0,1:T(8,128)}, f32[1024]{0:T(1024)}) all-reduce(f32[1024]{0:T(1024)S(1)} %reduce_sum.87, f32[32,16]{0,1:T(8,128)S(1)} %broadcast_multiply_fusion, f32[1024]{0:T(1024)S(1)} %get-tuple-element.60), channel_id=1, replica_groups=mesh['x'=2,'c'=2,'z'=4,'y'=2,'r'=1] {'x','c','z','y','r'}, use_global_device_ids=true, to_apply=%region_7.8 | all-reduce | flops 2560 | bytes 20480 | tf_op jit(solution)/shard_map/psum | solution.py:608
  334.7 91.9 %reduce-scatter.8.cloned.1.call-done = bf16[88,3072]{1,0:T(8,128)(2,1)} async-done(((bf16[704,3072]{1,0:T(8,128)(2,1)}), bf16[88,3072]{1,0:T(8,128)(2,1)}) %reduce-scatter.8.cloned.1.call-update) | async-done | bytes 540688 | tf_op jit(solution)/shard_map/reduce_scatter | solution.py:543
  (244 shorter events, 86.4 us)
Async XLA Ops:
  7.2 32.6 %all-gather.5.cloned.1.call-start = ((), (), s32[]{:S(2)}) async-start(), calls=%async_computation.5 | async-start | bytes 1310720 | tf_op jit(solution)/shard_map/all_gather | solution.py:430
  9.0 80.1 %all-gather.9.cloned.1.call-start = ((), (), s32[]{:S(2)}) async-start(), calls=%async_computation.10 | async-start | bytes 1310720 | tf_op jit(solution)/shard_map/all_gather | solution.py:432
  41.6 119.6 %all-gather.7.cloned.1.call-start = ((), (), s32[]{:S(2)}) async-start(), calls=%async_computation.6 | async-start | bytes 4866048 | tf_op jit(solution)/shard_map/all_gather | solution.py:438
  44.0 19.5 %collective-permute-start = (bf16[128,1024]{1,0:T(8,128)(2,1)S(1)}, bf16[128,1024]{1,0:T(8,128)(2,1)S(1)}, u32[]{:S(2)}, u32[]{:S(2)}) collective-permute-start(bf16[128,1024]{1,0:T(8,128)(2,1)S(1)} %fusion.20.refs_0_), channel_id=1, source_target_pairs={{0,2},{2,0},{4,6},{6,4},{1,3},{3,1},{5,7},{7,5},{8,10},{10,8},{12,... | collective-permute-start | bytes 786440 | tf_op jit(solution)/shard_map/ppermute | solution.py:46
  45.6 22.2 %collective-permute-start.1 = (bf16[128,1024]{1,0:T(8,128)(2,1)S(1)}, bf16[128,1024]{1,0:T(8,128)(2,1)S(1)}, u32[]{:S(2)}, u32[]{:S(2)}) collective-permute-start(bf16[128,1024]{1,0:T(8,128)(2,1)S(1)} %fusion.20.refs_0_), channel_id=1, source_target_pairs={{0,4},{2,6},{4,0},{6,2},{1,5},{3,7},{5,1},{7,3},{8,12},{10,14},{12... | collective-permute-start | bytes 786440 | tf_op jit(solution)/shard_map/ppermute | solution.py:46
  48.0 29.8 %collective-permute-start.2 = (bf16[128,1024]{1,0:T(8,128)(2,1)S(1)}, bf16[128,1024]{1,0:T(8,128)(2,1)S(1)}, u32[]{:S(2)}, u32[]{:S(2)}) collective-permute-start(bf16[128,1024]{1,0:T(8,128)(2,1)S(1)} %fusion.20.refs_0_), channel_id=1, source_target_pairs={{0,6},{2,4},{4,2},{6,0},{1,7},{3,5},{5,3},{7,1},{8,14},{10,12},{12... | collective-permute-start | bytes 786440 | tf_op jit(solution)/shard_map/ppermute | solution.py:46
  82.7 11.5 %collective-permute-start.4 = (bf16[768,128]{1,0:T(8,128)(2,1)}, bf16[768,128]{1,0:T(8,128)(2,1)S(1)}, u32[]{:S(2)}, u32[]{:S(2)}) collective-permute-start(bf16[768,128]{1,0:T(8,128)(2,1)} %get-tuple-element.37), channel_id=1, source_target_pairs={{0,1},{1,0},{16,17},{17,16},{2,3},{3,2},{18,19},{19,18},{4,5},{5,4... | collective-permute-start | bytes 589832 | tf_op jit(solution)/shard_map/ppermute | solution.py:46
  89.0 44.3 %collective-permute-start.8 = (bf16[4,128,1024]{2,1,0:T(8,128)(2,1)}, bf16[4,128,1024]{2,1,0:T(8,128)(2,1)S(1)}, u32[]{:S(2)}, u32[]{:S(2)}) collective-permute-start(bf16[4,128,1024]{2,1,0:T(8,128)(2,1)} %bitcast.66), channel_id=1, source_target_pairs={{0,8},{8,0},{1,9},{9,1},{2,10},{10,2},{3,11},{11,3},{4,12},{12,4},... | collective-permute-start | bytes 3145736 | tf_op jit(solution)/shard_map/ppermute | solution.py:46
  119.4 25.2 %all-to-all-start = ((bf16[16,64,128]{2,1,0:T(8,128)(2,1)}), bf16[16,64,128]{2,1,0:T(8,128)(2,1)S(1)}, u32[]{:S(2)}, u32[]{:S(2)}) async-start(bf16[16,64,128]{2,1,0:T(8,128)(2,1)} %get-tuple-element.40), calls=%async_computation | async-start | bytes 524288 | tf_op jit(solution)/shard_map/all_to_all | solution.py:502
  145.3 10.2 %collective-permute-start.11 = (bf16[128,1024]{1,0:T(8,128)(2,1)S(1)}, bf16[128,1024]{1,0:T(8,128)(2,1)S(1)}, u32[]{:S(2)}, u32[]{:S(2)}) collective-permute-start(bf16[128,1024]{1,0:T(8,128)(2,1)S(1)} %multiply_convert_fusion.2), channel_id=1, source_target_pairs={{0,17},{1,16},{16,1},{17,0},{2,19},{3,18},{18,3},{19,2},{4,21},{5,... | collective-permute-start | bytes 786440 | tf_op jit(solution)/shard_map/ppermute | solution.py:46
  145.9 13.4 %collective-permute-start.10 = (bf16[128,1024]{1,0:T(8,128)(2,1)S(1)}, bf16[128,1024]{1,0:T(8,128)(2,1)S(1)}, u32[]{:S(2)}, u32[]{:S(2)}) collective-permute-start(bf16[128,1024]{1,0:T(8,128)(2,1)S(1)} %multiply_convert_fusion.2), channel_id=1, source_target_pairs={{0,16},{1,17},{16,0},{17,1},{2,18},{3,19},{18,2},{19,3},{4,20},{5,... | collective-permute-start | bytes 786440 | tf_op jit(solution)/shard_map/ppermute | solution.py:46
  146.4 14.8 %collective-permute-start.9 = (bf16[128,1024]{1,0:T(8,128)(2,1)S(1)}, bf16[128,1024]{1,0:T(8,128)(2,1)}, u32[]{:S(2)}, u32[]{:S(2)}) collective-permute-start(bf16[128,1024]{1,0:T(8,128)(2,1)S(1)} %multiply_convert_fusion.2), channel_id=1, source_target_pairs={{0,1},{1,0},{16,17},{17,16},{2,3},{3,2},{18,19},{19,18},{4,5},{5,4... | collective-permute-start | bytes 786440 | tf_op jit(solution)/shard_map/ppermute | solution.py:46
  148.8 18.0 %collective-permute-start.17 = (bf16[128,1024]{1,0:T(8,128)(2,1)S(1)}, bf16[128,1024]{1,0:T(8,128)(2,1)}, u32[]{:S(2)}, u32[]{:S(2)}) collective-permute-start(bf16[128,1024]{1,0:T(8,128)(2,1)S(1)} %bitcast.69), channel_id=1, source_target_pairs={{0,17},{1,16},{16,1},{17,0},{2,19},{3,18},{18,3},{19,2},{4,21},{5,... | collective-permute-start | bytes 786440 | tf_op jit(solution)/shard_map/ppermute | solution.py:46
  149.4 19.3 %collective-permute-start.16 = (bf16[128,1024]{1,0:T(8,128)(2,1)S(1)}, bf16[128,1024]{1,0:T(8,128)(2,1)}, u32[]{:S(2)}, u32[]{:S(2)}) collective-permute-start(bf16[128,1024]{1,0:T(8,128)(2,1)S(1)} %bitcast.70), channel_id=1, source_target_pairs={{0,16},{1,17},{16,0},{17,1},{2,18},{3,19},{18,2},{19,3},{4,20},{5,... | collective-permute-start | bytes 786440 | tf_op jit(solution)/shard_map/ppermute | solution.py:46
  155.5 14.7 %collective-permute-start.15 = (bf16[128,1024]{1,0:T(8,128)(2,1)S(1)}, bf16[128,1024]{1,0:T(8,128)(2,1)}, u32[]{:S(2)}, u32[]{:S(2)}) collective-permute-start(bf16[128,1024]{1,0:T(8,128)(2,1)S(1)} %bitcast.71), channel_id=1, source_target_pairs={{0,1},{1,0},{16,17},{17,16},{2,3},{3,2},{18,19},{19,18},{4,5},{5,4... | collective-permute-start | bytes 786440 | tf_op jit(solution)/shard_map/ppermute | solution.py:46
  175.5 10.2 %collective-permute-start.20 = (bf16[128,1024]{1,0:T(8,128)(2,1)S(1)}, bf16[128,1024]{1,0:T(8,128)(2,1)S(1)}, u32[]{:S(2)}, u32[]{:S(2)}) collective-permute-start(bf16[128,1024]{1,0:T(8,128)(2,1)S(1)} %get-tuple-element.73), channel_id=1, source_target_pairs={{0,17},{1,16},{16,1},{17,0},{2,19},{3,18},{18,3},{19,2},{4,21},{5,... | collective-permute-start | bytes 786440 | tf_op jit(solution)/shard_map/ppermute | solution.py:46
  176.3 14.2 %collective-permute-start.19 = (bf16[128,1024]{1,0:T(8,128)(2,1)S(1)}, bf16[128,1024]{1,0:T(8,128)(2,1)S(1)}, u32[]{:S(2)}, u32[]{:S(2)}) collective-permute-start(bf16[128,1024]{1,0:T(8,128)(2,1)S(1)} %get-tuple-element.74), channel_id=1, source_target_pairs={{0,16},{1,17},{16,0},{17,1},{2,18},{3,19},{18,2},{19,3},{4,20},{5,... | collective-permute-start | bytes 786440 | tf_op jit(solution)/shard_map/ppermute | solution.py:46
  177.7 13.7 %collective-permute-start.18 = (bf16[128,1024]{1,0:T(8,128)(2,1)S(1)}, bf16[128,1024]{1,0:T(8,128)(2,1)S(1)}, u32[]{:S(2)}, u32[]{:S(2)}) collective-permute-start(bf16[128,1024]{1,0:T(8,128)(2,1)S(1)} %get-tuple-element.72), channel_id=1, source_target_pairs={{0,1},{1,0},{16,17},{17,16},{2,3},{3,2},{18,19},{19,18},{4,5},{5,4... | collective-permute-start | bytes 786440 | tf_op jit(solution)/shard_map/ppermute | solution.py:46
  180.1 16.8 %collective-permute-start.14 = (bf16[128,1024]{1,0:T(8,128)(2,1)S(1)}, bf16[128,1024]{1,0:T(8,128)(2,1)S(1)}, u32[]{:S(2)}, u32[]{:S(2)}) collective-permute-start(bf16[128,1024]{1,0:T(8,128)(2,1)S(1)} %get-tuple-element.76), channel_id=1, source_target_pairs={{0,17},{1,16},{16,1},{17,0},{2,19},{3,18},{18,3},{19,2},{4,21},{5,... | collective-permute-start | bytes 786440 | tf_op jit(solution)/shard_map/ppermute | solution.py:46
  180.9 18.7 %collective-permute-start.13 = (bf16[128,1024]{1,0:T(8,128)(2,1)S(1)}, bf16[128,1024]{1,0:T(8,128)(2,1)S(1)}, u32[]{:S(2)}, u32[]{:S(2)}) collective-permute-start(bf16[128,1024]{1,0:T(8,128)(2,1)S(1)} %get-tuple-element.77), channel_id=1, source_target_pairs={{0,16},{1,17},{16,0},{17,1},{2,18},{3,19},{18,2},{19,3},{4,20},{5,... | collective-permute-start | bytes 786440 | tf_op jit(solution)/shard_map/ppermute | solution.py:46
  185.6 15.9 %collective-permute-start.12 = (bf16[128,1024]{1,0:T(8,128)(2,1)S(1)}, bf16[128,1024]{1,0:T(8,128)(2,1)S(1)}, u32[]{:S(2)}, u32[]{:S(2)}) collective-permute-start(bf16[128,1024]{1,0:T(8,128)(2,1)S(1)} %get-tuple-element.75), channel_id=1, source_target_pairs={{0,1},{1,0},{16,17},{17,16},{2,3},{3,2},{18,19},{19,18},{4,5},{5,4... | collective-permute-start | bytes 786440 | tf_op jit(solution)/shard_map/ppermute | solution.py:46
  204.4 15.7 %all-to-all-start.1 = ((bf16[16,64,128]{2,1,0:T(8,128)(2,1)}), bf16[16,64,128]{2,1,0:T(8,128)(2,1)S(1)}, u32[]{:S(2)}, u32[]{:S(2)}) async-start(bf16[16,64,128]{2,1,0:T(8,128)(2,1)} %bitcast.18), calls=%async_computation.1 | async-start | bytes 524288 | tf_op jit(solution)/shard_map/all_to_all | solution.py:533
  208.3 83.1 %reduce-scatter.6.cloned.1.call-start = ((), (), s32[]{:S(2)}) async-start(), calls=%async_computation.8 | async-start | bytes 589824 | tf_op jit(solution)/shard_map/reduce_scatter | solution.py:601
  208.6 47.8 %collective-permute-start.31 = (bf16[128,1024]{1,0:T(8,128)(2,1)S(1)}, bf16[128,1024]{1,0:T(8,128)(2,1)S(1)}, u32[]{:S(2)}, u32[]{:S(2)}) collective-permute-start(bf16[128,1024]{1,0:T(8,128)(2,1)S(1)} %get-tuple-element.65.refs_4_), channel_id=1, source_target_pairs={{0,2},{2,0},{4,6},{6,4},{1,3},{3,1},{5,7},{7,5},{8,10},{10,8},{12,... | collective-permute-start | bytes 786440 | tf_op jit(solution)/shard_map/ppermute | solution.py:46
  210.5 45.8 %collective-permute-start.32 = (bf16[128,1024]{1,0:T(8,128)(2,1)S(1)}, bf16[128,1024]{1,0:T(8,128)(2,1)}, u32[]{:S(2)}, u32[]{:S(2)}) collective-permute-start(bf16[128,1024]{1,0:T(8,128)(2,1)S(1)} %get-tuple-element.65.refs_4_), channel_id=1, source_target_pairs={{0,4},{2,6},{4,0},{6,2},{1,5},{3,7},{5,1},{7,3},{8,12},{10,14},{12... | collective-permute-start | bytes 786440 | tf_op jit(solution)/shard_map/ppermute | solution.py:46
  212.9 43.5 %collective-permute-start.33 = (bf16[128,1024]{1,0:T(8,128)(2,1)S(1)}, bf16[128,1024]{1,0:T(8,128)(2,1)}, u32[]{:S(2)}, u32[]{:S(2)}) collective-permute-start(bf16[128,1024]{1,0:T(8,128)(2,1)S(1)} %get-tuple-element.65.refs_4_), channel_id=1, source_target_pairs={{0,6},{2,4},{4,2},{6,0},{1,7},{3,5},{5,3},{7,1},{8,14},{10,12},{12... | collective-permute-start | bytes 786440 | tf_op jit(solution)/shard_map/ppermute | solution.py:46
  241.7 18.1 %collective-permute-start.21 = (bf16[2048,128]{1,0:T(8,128)(2,1)}, bf16[2048,128]{1,0:T(8,128)(2,1)S(1)}, u32[]{:S(2)}, u32[]{:S(2)}) collective-permute-start(bf16[2048,128]{1,0:T(8,128)(2,1)} %get-tuple-element.47), channel_id=1, source_target_pairs={{0,8},{8,0},{1,9},{9,1},{2,10},{10,2},{3,11},{11,3},{4,12},{12,4},... | collective-permute-start | bytes 1572872 | tf_op jit(solution)/shard_map/ppermute | solution.py:46
  259.7 73.3 %reduce-scatter.4.cloned.1.call-start = ((), (), s32[]{:S(2)}) async-start(), calls=%async_computation.7 | async-start | bytes 1769472 | tf_op jit(solution)/shard_map/reduce_scatter | solution.py:602
  275.7 150.8 %reduce-scatter.8.cloned.1.call-start = ((), (), s32[]{:S(2)}) async-start(), calls=%async_computation.9 | async-start | bytes 4866048 | tf_op jit(solution)/shard_map/reduce_scatter | solution.py:543
  285.4 46.3 %collective-permute-start.27 = (bf16[128,1024]{1,0:T(8,128)(2,1)S(1)}, bf16[128,1024]{1,0:T(8,128)(2,1)S(1)}, u32[]{:S(2)}, u32[]{:S(2)}) collective-permute-start(bf16[128,1024]{1,0:T(8,128)(2,1)S(1)} %copy-done.44), channel_id=1, source_target_pairs={{0,6},{2,4},{4,2},{6,0},{1,7},{3,5},{5,3},{7,1},{8,14},{10,12},{12... | collective-permute-start | bytes 786440 | tf_op jit(solution)/shard_map/ppermute | solution.py:46
  285.4 46.3 %collective-permute-start.26 = (bf16[128,1024]{1,0:T(8,128)(2,1)S(1)}, bf16[128,1024]{1,0:T(8,128)(2,1)S(1)}, u32[]{:S(2)}, u32[]{:S(2)}) collective-permute-start(bf16[128,1024]{1,0:T(8,128)(2,1)S(1)} %copy-done.43), channel_id=1, source_target_pairs={{0,4},{2,6},{4,0},{6,2},{1,5},{3,7},{5,1},{7,3},{8,12},{10,14},{12... | collective-permute-start | bytes 786440 | tf_op jit(solution)/shard_map/ppermute | solution.py:46
  287.0 44.6 %collective-permute-start.25 = (bf16[128,1024]{1,0:T(8,128)(2,1)S(1)}, bf16[128,1024]{1,0:T(8,128)(2,1)S(1)}, u32[]{:S(2)}, u32[]{:S(2)}) collective-permute-start(bf16[128,1024]{1,0:T(8,128)(2,1)S(1)} %copy-done.42), channel_id=1, source_target_pairs={{0,2},{2,0},{4,6},{6,4},{1,3},{3,1},{5,7},{7,5},{8,10},{10,8},{12,... | collective-permute-start | bytes 786440 | tf_op jit(solution)/shard_map/ppermute | solution.py:46
  (61 other events, 714.1 us)
Sparse Core Ops, SparseCore 0:
  10.5 29.3 all-gather.4
  42.0 47.0 all-gather.8
  90.6 47.5 all-gather.6
  259.8 30.6 reduce-scatter.5
  294.0 38.9 reduce-scatter.3
  335.3 91.2 reduce-scatter.7

commit v2 on v1

--- a/solution.py
+++ b/solution.py
@@ -15,8 +15,7 @@
 BF16 = jnp.bfloat16
 VMEM_LIMIT = 60 * 1024 * 1024
 SQUARE = ("x", "y")
-HEADS_GROUP = ("x", "c", "y", "r")
-UNITS_GROUP = ("c", "z", "r")
+UNITS_GROUP = ("z", "c", "r")
 EVERY = ("x", "c", "z", "y", "r")
 
 
@@ -54,7 +53,12 @@
     return [values[0]] + [swap(values[mask], axis, mask) for mask in (1, 2, 3)]
 
 
-def kernel_call(body, out_shapes, inputs, scratch=(), scalars=1):
+def sum_everywhere(value, axis):
+    first, second, third, fourth = from_group(value, axis)
+    return (first + second) + (third + fourth)
+
+
+def kernel_call(body, out_shapes, inputs, scratch=(), scalars=1, micros=4):
     in_specs = [pl.BlockSpec(memory_space=pltpu.SMEM)] * scalars
     in_specs += [pl.BlockSpec(memory_space=pltpu.VMEM)] * (len(inputs) - scalars)
     return pl.pallas_call(
@@ -64,6 +68,9 @@
         out_specs=jax.tree.map(lambda _: pl.BlockSpec(memory_space=pltpu.VMEM), out_shapes),
         scratch_shapes=list(scratch),
         compiler_params=pltpu.CompilerParams(vmem_limit_bytes=VMEM_LIMIT),
+        cost_estimate=pl.CostEstimate(
+            flops=int(micros * 1.15e9), bytes_accessed=1 << 20, transcendentals=0
+        ),
     )(*inputs)
 
 
@@ -72,24 +79,22 @@
 
 
 def qkv_body(hd, coords, *refs):
-    blocks, (wa, wb), pieces = refs[:4], refs[4:6], refs[6:10]
-    rows_all, weights = refs[10:12]
-    x_at, c_at, y_at = coords[0], coords[1], coords[3]
+    blocks, parts, other_rows, pieces = refs[:4], refs[4:8], refs[8], refs[9:13]
+    rows_all, weights = refs[13:15]
+    c_at, y_at = coords[1], coords[3]
     tokens, width = blocks[0].shape
+    half = hd // 2
     for at in range(4):
         rows_all[at * tokens : (at + 1) * tokens, :] = blocks[at][...]
-    for dest in range(4):
-        base = pl.multiple_of((x_at ^ (dest >> 1)) * hd, hd)
-        other = (y_at ^ (dest & 1)) ^ c_at
-
-        def put(source, base=base, dest=dest):
-            for kind, start in ((0, 8 * hd + dest * hd), (1, dest * 2 * hd), (2, dest * 2 * hd + hd)):
-                weights[start : start + hd, :] = source[
-                    pl.ds(base, hd), kind * width : (kind + 1) * width
-                ]
-
-        pl.when(other == 0)(functools.partial(put, wa))
-        pl.when(other == 1)(functools.partial(put, wb))
+    for core in range(2):
+        for dest in range(4):
+            column = y_at ^ c_at ^ core
+            place = (dest >> 1) * 2 + column
+            shift = pl.multiple_of((y_at ^ (dest & 1)) * half, half)
+            source = other_rows.at[dest * half : (dest + 1) * half] if core else parts[dest]
+            for kind, first, step in ((0, 8 * hd, hd), (1, 0, 2 * hd), (2, hd, 2 * hd)):
+                start = pl.multiple_of(first + place * step + shift, half)
+                weights[pl.ds(start, half), :] = source[:, kind * width : (kind + 1) * width]
     normed = rows_all[...]
     pairs = nt(normed, weights[0 : 8 * hd, :]).astype(BF16)
     queries = nt(weights[8 * hd : 12 * hd, :], normed).astype(BF16)
@@ -148,7 +153,7 @@
         own, other, refs = refs[:4], refs[4:8], refs[8:]
     else:
         refs = refs[12:]
-    out, out_near, lse, attended, keys, keys_t, queries, scores, bias = refs
+    out, lse, attended, keys, keys_t, queries, scores, bias = refs
     x_at, c_at, z_at, y_at, r_at = (coords[at] for at in range(5))
     block = 4 * tokens
     for dest in range(4):
@@ -222,7 +227,6 @@
         for half in range(2):
             part = low[:, half * tokens : (half + 1) * tokens]
             out[half * 8 + y_to * 4 + z_to] = part
-            out_near[((x_at ^ half) * 2 + (y_to ^ y_at)) * 4 + (z_to ^ z_at)] = part
         return carry
 
     lax.fori_loop(0, queries.shape[0], one_block, 0)
@@ -340,11 +344,10 @@
 
 
 def project_back_body(hd, coords, *refs):
-    pieces, (rows_all, weights, gain), outs = refs[:4], refs[4:7], refs[7:11]
-    weight_out, gain_out = refs[11:13]
-    pairs, pairs_t, queries, queries_t = refs[13:]
-    x_at, c_at, y_at = coords[0], coords[1], coords[3]
-    tokens, width = outs[0].shape
+    pieces, (rows_all, weights, gain), out = refs[:4], refs[4:7], refs[7]
+    gain_out, pairs_t, queries_t, pairs, queries = refs[8:]
+    tokens, width = out.shape[1:]
+    z_at = coords[2]
     for dest in range(4):
         lanes = slice(dest * 2 * hd, (dest + 1) * 2 * hd)
         part = pieces[dest][0 : 4 * tokens, :]
@@ -355,38 +358,71 @@
                 4 * tokens + at * hd : 4 * tokens + (at + 1) * hd, :
             ]
     queries[...] = queries_t[...].T
-    normed = rows_all[...]
     grad = nn(pairs[...], weights[0 : 8 * hd, :]) + nn(queries[...], weights[8 * hd :, :])
-    unit = normed.astype(F32) / gain[...]
+    unit = rows_all[...].astype(F32) / gain[...]
     gain_out[...] = fold_rows(grad * unit, jnp.sum)
     for at in range(4):
-        outs[at][...] = grad[at * tokens : (at + 1) * tokens, :].astype(BF16)
+        out[z_at ^ at] = grad[at * tokens : (at + 1) * tokens, :].astype(BF16)
+
+
+def head_grads_body(hd, coords, pairs_t, queries_t, rows_all, keep, send):
+    c_at, y_at = coords[1], coords[3]
+    width = rows_all.shape[1]
+    half = hd // 2
+    normed = rows_all[...]
     pair_rows = nn(pairs_t[...], normed).astype(BF16)
     query_rows = nn(queries_t[...], normed).astype(BF16)
     for dest in range(4):
-        head = (x_at ^ (dest >> 1)) * 2 + (y_at ^ (dest & 1))
-        rows = pl.ds(pl.multiple_of(head * hd, hd), hd)
-        weight_out[rows, 0:width] = query_rows[dest * hd : (dest + 1) * hd, :]
-        start = dest * 2 * hd
-        weight_out[rows, width : 2 * width] = pair_rows[start : start + hd, :]
-        weight_out[rows, 2 * width : 3 * width] = pair_rows[start + hd : start + 2 * hd, :]
-
-
-def output_back_body(hd, coords, *refs):
-    pieces, blocks, weight_out, rows_all, features = refs[:4], refs[4:8], refs[8], refs[9], refs[10]
+        other = (y_at ^ (dest & 1)) ^ c_at
+
+        def put(target, dest=dest):
+            for part in range(2):
+                place = (dest >> 1) * 2 + (y_at ^ part)
+                for kind, rows, first in (
+                    (0, query_rows, dest * hd),
+                    (1, pair_rows, dest * 2 * hd),
+                    (2, pair_rows, dest * 2 * hd + hd),
+                ):
+                    first += part * half
+                    target[place, :, kind * width : (kind + 1) * width] = rows[
+                        first : first + half, :
+                    ]
+
+        pl.when(other == 0)(functools.partial(put, keep))
+        pl.when(other == 1)(functools.partial(put, send))
+
+
+def output_body(hd, coords, *refs):
+    arrived, own_in, gain, parts, middle_out, normed_out, weights, features = refs
     x_at, y_at = coords[0], coords[3]
-    tokens = blocks[0].shape[0]
-    for at in range(4):
-        rows_all[at * tokens : (at + 1) * tokens, :] = blocks[at][...]
+    half, tokens = hd // 2, arrived.shape[1]
+    for z_of in range(4):
+        for c_of in range(2):
+            for dest in range(4):
+                head = ((x_at ^ (dest >> 1)) * 2 + c_of) * 4 + z_of
+                start = pl.multiple_of(head * hd + (y_at ^ (dest & 1)) * half, half)
+                weights[pl.ds(start, half), :] = parts[
+                    z_of * 2 + c_of, dest * half : (dest + 1) * half, :
+                ]
     for dest in range(4):
-        for at in range(4):
-            features[dest * hd : (dest + 1) * hd, at * tokens : (at + 1) * tokens] = pieces[dest][at]
-    result = nn(features[...], rows_all[...]).astype(BF16)
-    for dest in range(4):
-        head = (x_at ^ (dest >> 1)) * 2 + (y_at ^ (dest & 1))
-        weight_out[pl.ds(pl.multiple_of(head * hd, hd), hd), :] = result[
-            dest * hd : (dest + 1) * hd, :
-        ]
+        for z_of in range(4):
+            for c_of in range(2):
+                head = ((x_at ^ (dest >> 1)) * 2 + c_of) * 4 + z_of
+                start = pl.multiple_of(head * hd + (y_at ^ (dest & 1)) * half, half)
+                lanes = slice((z_of * 2 + c_of) * tokens, (z_of * 2 + c_of + 1) * tokens)
+                features[dest, :, lanes] = arrived[pl.ds(start, half), :]
+    middle = own_in[...].astype(F32) + nn(arrived[...].T, weights[...])
+    middle_out[...] = middle
+    normed_out[...] = (middle * norm_scale(middle) * gain[...]).astype(BF16)
+
+
+def finish_body(*refs):
+    parts, own_in, grad_middle, gain, out = refs
+    values = own_in[...].astype(F32)
+    grad = sum(parts[at].astype(F32) for at in range(4))
+    out[...] = (
+        grad_middle[...] + norm_back(values, norm_scale(values), gain[...], grad)
+    ).astype(BF16)
 
 
 def gated(gate_act, up_act):
@@ -427,19 +463,16 @@
     normed_parts = from_group(normed, "z")
 
     joined = jnp.concatenate([query_weight, key_weight, value_weight, output_weight], axis=1)
-    head_rows = lax.all_gather(joined, ("x", "y", "r"), axis=0, tiled=True)
-    head_rows_other = swap(head_rows, "c", 1)
-    out_z = lax.all_gather(head_rows[:, 3 * width :], "z", axis=0, tiled=False)
-    out_z_other = swap(out_z, "c", 1)
-    out_first = jnp.where(c_at == 0, out_z, out_z_other).reshape(4, 2, hd, width)
-    out_second = jnp.where(c_at == 0, out_z_other, out_z).reshape(4, 2, hd, width)
-    out_full = jnp.stack([out_first, out_second]).transpose(2, 0, 1, 3, 4).reshape(width, width)
+    if repeat > 1:
+        joined = lax.all_gather(joined, "r", axis=0, tiled=True)
+    head_rows = from_group(joined, SQUARE)
+    other_rows = swap(jnp.concatenate([part[:, : 3 * width] for part in head_rows]), "c", 1)
+    out_rows = jnp.concatenate([part[:, 3 * width :] for part in head_rows])
     units = jnp.concatenate([gate_weight, up_weight, down_weight], axis=1)
     unit_rows = lax.all_gather(units, UNITS_GROUP, axis=0, tiled=True)
     gate_piece, up_piece, down_piece = (
         unit_rows[:, at * width : (at + 1) * width] for at in range(3)
     )
-    cot_all = jnp.concatenate(from_group(cot_own, SQUARE), axis=0)
 
     windows = segment_ids.reshape(-1, 2 * tokens)
     cuts = jnp.sum((windows < windows[:, -1:]).astype(jnp.int32), axis=1)
@@ -463,14 +496,19 @@
     diag = jnp.dot(onehot, bias_col, precision=HIGHEST) - jnp.sum(far_onehot * bias_col)
     hvec = jnp.pad(diag.reshape(3, 2 * reach), ((0, 5), (0, 0)))
 
+    normed_parts, hvec, cuts, coords, out_rows = lax.optimization_barrier(
+        (normed_parts, hvec, cuts, coords, out_rows)
+    )
     made = kernel_call(
         functools.partial(qkv_body, hd),
         [shape((block + 4 * hd, 2 * hd), BF16)] * 4
         + [shape((block, width), BF16), shape((12 * hd, width), BF16)],
-        [coords, *normed_parts, head_rows[:, : 3 * width], head_rows_other[:, : 3 * width]],
+        [coords, *normed_parts, *head_rows, other_rows],
     )
     pieces, (normed_all, group_weights) = made[:4], made[4:]
     pieces = to_group(pieces, SQUARE)
+
+    out_all = lax.all_gather(out_rows, ("z", "c"), axis=0, tiled=False)
     own = [piece[:block] for piece in pieces]
     other = swap(jnp.concatenate(own, axis=0), "c", 1)
     other = [other[at * block : (at + 1) * block] for at in range(4)]
@@ -481,10 +519,9 @@
         other = [lax.all_gather(part, "r", axis=0, tiled=True) for part in other]
         arrays = [*pieces, *own, *other]
     places = 8
-    out_t, out_near, lse, attended, keys, keys_t, queries = kernel_call(
+    out_t, lse, attended, keys, keys_t, queries = kernel_call(
         functools.partial(attend_body, tokens, hd, repeat),
         [
-            shape((16, hd, tokens), BF16),
             shape((16, hd, tokens), BF16),
             shape((places, 8, 2 * tokens), F32),
             shape((places, hd, 2 * tokens), F32),
@@ -498,15 +535,30 @@
             pltpu.VMEM((2 * block, 2 * tokens), F32),
         ],
         scalars=2,
-    )
+        micros=20,
+    )
+    cot_sent, _ = lax.optimization_barrier((cot_own, other))
+    cot_parts, out_t = lax.optimization_barrier((from_group(cot_sent, SQUARE), out_t))
+    cot_all = jnp.concatenate(cot_parts, axis=0)
     arrived = lax.all_to_all(out_t, ("x", "y", "z"), split_axis=0, concat_axis=0, tiled=True)
-    near = to_group(
-        [out_near[4 * at : 4 * at + 4].reshape(4 * hd, tokens) for at in range(4)], SQUARE
-    )
-
-    middle = hidden_in + tn(arrived.reshape(width, tokens), out_full)
+
+    middle, normed_mid, out_full, features = kernel_call(
+        functools.partial(output_body, hd),
+        [
+            shape((tokens, width), F32),
+            shape((tokens, width), BF16),
+            shape((width, width), BF16),
+            shape((4, hd // 2, 8 * tokens), BF16),
+        ],
+        [
+            coords,
+            arrived.reshape(width, tokens),
+            inputs[0],
+            gain_feedforward.reshape(1, width),
+            out_all,
+        ],
+    )
     scale_second = norm_scale(middle)
-    normed_mid = (middle * scale_second * gain_feedforward).astype(BF16)
     mid_all = jnp.concatenate(from_group(normed_mid, SQUARE), axis=0)
 
     gate_act = nt(mid_all, gate_piece)
@@ -519,10 +571,12 @@
     grad_parts = to_group(
         [grad_norm[at * tokens : (at + 1) * tokens] for at in range(4)], SQUARE
     )
+    unit_grads = jnp.concatenate(
+        [tn(gate_low, mid_all), tn(up_low, mid_all), tn(hidden, cot_all)], axis=1
+    ).astype(BF16)
+    feed = nn(hidden, down_piece).astype(BF16)
+    grad_parts, unit_grads, feed = lax.optimization_barrier((grad_parts, unit_grads, feed))
     grad_norm_mid = sum(part.astype(F32) for part in grad_parts)
-    feed = nn(hidden, down_piece).astype(BF16)
-    feed_parts = to_group([feed[at * tokens : (at + 1) * tokens] for at in range(4)], SQUARE)
-    layer_out = (middle + sum(part.astype(F32) for part in feed_parts)).astype(BF16)
 
     grad_middle = cot_own.astype(F32) + norm_back(
         middle, scale_second, gain_feedforward, grad_norm_mid
@@ -537,10 +591,23 @@
         concat_axis=0,
         tiled=True,
     )
-    unit_grads = jnp.concatenate(
-        [tn(gate_low, mid_all), tn(up_low, mid_all), tn(hidden, cot_all)], axis=1
-    ).astype(BF16)
-    unit_grads = lax.psum_scatter(unit_grads, UNITS_GROUP, scatter_dimension=0, tiled=True)
+    grad_arrived, grad_mid_low, unit_grads = lax.optimization_barrier(
+        (grad_arrived, grad_mid_low, unit_grads)
+    )
+    grad_units = lax.psum_scatter(unit_grads, UNITS_GROUP, scatter_dimension=0, tiled=True)
+    mixed = to_group(
+        [
+            jnp.concatenate(
+                [
+                    feed[at * tokens : (at + 1) * tokens],
+                    grad_mid_low,
+                    features[at],
+                ]
+            )
+            for at in range(4)
+        ],
+        SQUARE,
+    )
 
     grad_own, grad_other, grad_q, table_out, far_out = kernel_call(
         functools.partial(attend_back_body, tokens, hd, repeat),
@@ -558,7 +625,9 @@
             pltpu.VMEM((2 * block, 2 * tokens), F32),
         ],
         scalars=2,
-    )
+        micros=20,
+    )
+    mixed, grad_own = lax.optimization_barrier((mixed, grad_own))
     grad_pairs = (grad_own + swap(grad_other, "c", 1).astype(F32)).astype(BF16)
     grad_pairs = [
         grad_pairs[at * repeat * block : (at + 1) * repeat * block] for at in range(4)
@@ -571,45 +640,67 @@
         jnp.concatenate([grad_pairs[at], grad_q[4 * at : 4 * at + 4].reshape(4 * hd, tokens)])
         for at in range(4)
     ]
+    mixed, grad_pieces = lax.optimization_barrier((mixed, grad_pieces))
     grad_pieces = to_group(grad_pieces, SQUARE)
 
     made = kernel_call(
         functools.partial(project_back_body, hd),
-        [shape((tokens, width), BF16)] * 4
-        + [shape((4 * hd, 3 * width), BF16), shape((8, width), F32)],
+        [
+            shape((4, tokens, width), BF16),
+            shape((8, width), F32),
+            shape((8 * hd, block), BF16),
+            shape((4 * hd, block), BF16),
+        ],
         [coords, *grad_pieces, normed_all, group_weights, gain_attention.reshape(1, width)],
-        [
-            pltpu.VMEM((block, 8 * hd), BF16),
-            pltpu.VMEM((8 * hd, block), BF16),
-            pltpu.VMEM((block, 4 * hd), BF16),
-            pltpu.VMEM((4 * hd, block), BF16),
-        ],
-    )
-    normed_grads, head_grads, gain_first_rows = made[:4], made[4], made[5]
-    grad_normed = sum(part.astype(F32) for part in to_group(normed_grads, "z"))
-    grad_inputs = (
-        grad_middle + norm_back(hidden_in, scale_first, gain_attention, grad_normed)
-    ).astype(BF16)
-
-    mid_parts = from_group(grad_mid_low, "z")
-    out_grads = kernel_call(
-        functools.partial(output_back_body, hd),
-        shape((4 * hd, width), BF16),
-        [coords, *[part.reshape(4, hd, tokens) for part in near], *mid_parts],
-        [pltpu.VMEM((block, width), BF16), pltpu.VMEM((4 * hd, block), BF16)],
-    )
-    out_grads = lax.psum_scatter(out_grads, HEADS_GROUP, scatter_dimension=0, tiled=True)
-    head_grads = lax.psum_scatter(head_grads, HEADS_GROUP, scatter_dimension=0, tiled=True)
-
+        [pltpu.VMEM((block, 8 * hd), BF16), pltpu.VMEM((block, 4 * hd), BF16)],
+    )
+    normed_grads, gain_first_rows, pairs_t, queries_t = made
+    normed_grads = lax.all_to_all(normed_grads, "z", split_axis=0, concat_axis=0, tiled=True)
+    keep, send = kernel_call(
+        functools.partial(head_grads_body, hd),
+        [shape((4, hd // 2, 3 * width), BF16)] * 2,
+        [coords, pairs_t, queries_t, normed_all],
+    )
+    layer_out = (middle + sum(part[:tokens].astype(F32) for part in mixed)).astype(BF16)
+    grad_mid_all = jnp.concatenate([part[tokens : 2 * tokens] for part in mixed], axis=0)
+    near = jnp.stack([part[2 * tokens :] for part in mixed]).reshape(4, hd // 2, 8, tokens)
+    near = near.transpose(2, 1, 0, 3).reshape(4 * hd, block)
+    out_grads = nn(near, grad_mid_all).astype(BF16)
+
+    table_out, far_out, keep, send, grad_units, out_grads = lax.optimization_barrier(
+        (table_out, far_out, keep, send, grad_units, out_grads)
+    )
+    out_grads = lax.psum_scatter(out_grads, UNITS_GROUP, scatter_dimension=0, tiled=True)
+    head_grads = (keep.astype(F32) + swap(send, "c", 1).astype(F32)).astype(BF16)
     bucket_grad = jnp.dot(table_out[:3].reshape(1, -1), onehot, precision=HIGHEST)[0]
     bucket_grad = bucket_grad + far_onehot * jnp.sum(far_out)
     head_mark = (jnp.arange(head_count) == head_at).astype(F32)
     bias_term = bucket_grad[:, None] * head_mark[None, :]
-    gain_first_grad, gain_second_grad, bias_grad = lax.psum(
-        (jnp.sum(gain_first_rows, axis=0), gain_second_term, bias_term), EVERY
-    )
-    head_grads = head_grads.astype(F32)
-    unit_grads = unit_grads.astype(F32)
+    sums = jnp.concatenate([jnp.sum(gain_first_rows, axis=0), gain_second_term, bias_term.ravel()])
+    sums = sums + swap(sums, "c", 1)
+    sums = sum_everywhere(sums, SQUARE)
+    normed_grads, head_grads, sums = lax.optimization_barrier((normed_grads, head_grads, sums))
+    sums = sum_everywhere(sums, "z")
+    head_grads = to_group([head_grads[at] for at in range(4)], SQUARE)
+    head_grads = sum(part.astype(F32) for part in head_grads)
+    if repeat > 1:
+        head_grads = lax.psum_scatter(
+            head_grads.astype(BF16), "r", scatter_dimension=0, tiled=True
+        ).astype(F32)
+
+    if repeat > 1:
+        sums = lax.psum(sums, "r")
+    gain_first_grad, gain_second_grad = sums[:width], sums[width : 2 * width]
+    bias_grad = sums[2 * width :].reshape(bucket_count, head_count)
+
+    grad_inputs = kernel_call(
+        finish_body,
+        shape((tokens, width), BF16),
+        [normed_grads, inputs[0], grad_middle, gain_attention.reshape(1, width)],
+        scalars=0,
+        micros=100,
+    )
+    unit_grads = grad_units.astype(F32)
     return (
         layer_out[None],
         grad_inputs[None],

time: 436 us -> 269 us (0.62)
  waiting for transfers between devices: 222 us -> 65.4 us
  blocking collectives: 38.7 us -> 12.6 us
  other arithmetic: 16.7 us -> 23.5 us
  Pallas kernels: 52.5 us -> 59.2 us
    reduce_scatter x1, waiting for transfers between devices: 91.9 us -> 0.01 us  [body(): lax.psum_scatter(unit_grads, UNITS_GROUP, scatter_dimension=0, tiled=True)]
    ppermute x34 -> x38, waiting for transfers between devices: 78.4 us -> 35.1 us  [swap(): return lax.ppermute(value, axis, [(at, at ^ mask) for at in range(size)])]
    psum x1 -> x0, blocking collectives: 38.7 us -> none  [body(): lax.psum((jnp.sum(gain_first_rows, axis=0), gain_second_term, bias_term),...]
    all_gather x2 -> x1, waiting for transfers between devices: 33.6 us -> 0.01 us  [body(): out_all = lax.all_gather(out_rows, ('z', 'c'), axis=0, tiled=False)]
    all_to_all x0 -> x1, blocking collectives: none -> 12.6 us  [body(): lax.all_to_all(grad_attended.reshape(16, hd, tokens), ('x', 'y', 'z'), sp...]
    ppermute x34 -> x38, starting transfers between devices: 33.1 us -> 42.8 us  [swap(): return lax.ppermute(value, axis, [(at, at ^ mask) for at in range(size)])]
    all_to_all x1, waiting for transfers between devices: 10.7 us -> 18.3 us  [body(): lax.all_to_all(out_t, ('x', 'y', 'z'), split_axis=0, concat_axis=0, tiled...]
    all_to_all x1, starting transfers between devices: 13.9 us -> 6.77 us  [body(): lax.all_to_all(out_t, ('x', 'y', 'z'), split_axis=0, concat_axis=0, tiled...]
  transfers between devices with their start and end apart: 42 -> 44, of which waited for: 26 -> 20; matrix products, arithmetic and copies ran while one was open for 9% -> 15% of each run, Pallas kernels for 12% -> 22%
where the time goes in v2:
time: 269 us; the launch traced here: 267 us
  waiting for transfers between devices  65.4 us (24%)
  Pallas kernels  59.2 us (22%)
  starting transfers between devices  53.6 us (20%)
  other arithmetic  23.5 us (9%)
  local copies, waits for them, and re-layouts  20.6 us (8%)
  matrix products  17.3 us (6%)
  between operations  14.9 us (6%)
  blocking collectives  12.6 us (5%)
    pallas_call x7, Pallas kernels, kernel_call(): pl.pallas_call(body, out_shape=out_shapes, in_specs=in_specs, out_specs=j...  59.2 us
    ppermute x38, starting transfers between devices, swap(): return lax.ppermute(value, axis, [(at, at ^ mask) for at in range(size)])  42.8 us
    ppermute x38, waiting for transfers between devices, swap(): return lax.ppermute(value, axis, [(at, at ^ mask) for at in range(size)])  35.1 us
    all_to_all x1, waiting for transfers between devices, body(): lax.all_to_all(out_t, ('x', 'y', 'z'), split_axis=0, concat_axis=0, tiled...  18.3 us
    all_to_all x1, blocking collectives, body(): lax.all_to_all(grad_attended.reshape(16, hd, tokens), ('x', 'y', 'z'), sp...  12.6 us
    all_to_all x1, waiting for transfers between devices, body(): lax.all_to_all(normed_grads, 'z', split_axis=0, concat_axis=0, tiled=True)  11.9 us
    unnamed x114, local copies, waits for them, and re-layouts  8.7 us
    all_to_all x1, starting transfers between devices, body(): lax.all_to_all(out_t, ('x', 'y', 'z'), split_axis=0, concat_axis=0, tiled...  6.77 us
  transfers between devices with their start and end apart: 44, of which 20 were waited for; matrix products, arithmetic and copies ran while one was open for 15% of the time, Pallas kernels for 22%

profile of v2, /device:TPU:0, one launch (start us, length us, event | category | flops | bytes accessed | tf_op | source)
XLA Modules:
  0.0 267.1 jit_solution(12432005823409947967)
XLA Ops:
  9.6 3.1 %collective-permute-start = (bf16[128,1024]{1,0:T(8,128)(2,1)S(1)}, bf16[128,1024]{1,0:T(8,128)(2,1)S(1)}, u32[]{:S(2)}, u32[]{:S(2)}) collective-permute-start(bf16[128,1024]{1,0:T(8,128)(2,1)S(1)} %fusion.31.refs_0_), channel_id=1, source_target_pairs={{0,2},{2,0},{4,6},{6,4},{1,3},{3,1},{5,7},{7,5},{8,10},{10,8},{12,... | collective-permute-start | bytes 786440 | tf_op jit(solution)/shard_map/ppermute | solution.py:45
  12.7 2.6 collective-permute-start.1
  18.7 2.7 collective-permute-start.5
  33.3 2.0 collective-permute-done.3.refs_5_
  37.6 2.3 collective-permute-done.6.refs_8_
  40.8 4.1 %shard_map.229 = (bf16[768,128]{1,0:T(8,128)(2,1)}, bf16[768,128]{1,0:T(8,128)(2,1)}, bf16[768,128]{1,0:T(8,128)(2,1)}, bf16[768,128]{1,0:T(8,128)(2,1)}, bf16[5...) custom-call(s32[5]{0:T(128)} %stack.35.coords, bf16[128,1024]{1,0:T(8,128)(2,1)} %copy-done.10, ...), custom_call_target="tpu_custom_call" | custom-call | flops 4600000000 | bytes 1048576 | tf_op jit(solution)/shard_map/pallas_call | solution.py:64
  44.8 2.5 collective-permute-start.9
  49.3 4.5 %collective-permute-done.9.refs_3_ = bf16[768,128]{1,0:T(8,128)(2,1)S(1)} collective-permute-done((bf16[768,128]{1,0:T(8,128)(2,1)}, bf16[768,128]{1,0:T(8,128)(2,1)S(1)}, u32[]{:S(2)}, u32[]{:S(2)}) %collective-permute-start.9) | collective-permute-done | bytes 196640 | tf_op jit(solution)/shard_map/ppermute | solution.py:45
  53.8 3.5 %collective-permute-done.8.refs_2_ = bf16[768,128]{1,0:T(8,128)(2,1)S(1)} collective-permute-done((bf16[768,128]{1,0:T(8,128)(2,1)}, bf16[768,128]{1,0:T(8,128)(2,1)S(1)}, u32[]{:S(2)}, u32[]{:S(2)}) %collective-permute-start.8) | collective-permute-done | bytes 196640 | tf_op jit(solution)/shard_map/ppermute | solution.py:45
  63.7 19.6 %shard_map.230 = (bf16[16,64,128]{2,1,0:T(8,128)(2,1)}, f32[8,8,256]{2,1,0:T(8,128)}, f32[8,64,256]{2,1,0:T(8,128)}, bf16[4096,128]{1,0:T(8,128)(2,1)}, bf16[8,1...) custom-call(s32[5]{0:T(128)} %stack.35.coords, s32[16]{0:T(128)} %convert_reduce_fusion.cuts, f32[8,256]{1,0:T(8,128)} %pad.4.hvec, ...), custom_call_target="tpu_custom_call" | custom-call | flops 23000000512 | bytes 1048576 | tf_op jit(solution)/shard_map/pallas_call | solution.py:64
  83.3 6.8 %all-to-all-start = ((bf16[16,64,128]{2,1,0:T(8,128)(2,1)}), bf16[16,64,128]{2,1,0:T(8,128)(2,1)S(1)}, u32[]{:S(2)}, u32[]{:S(2)}) async-start(bf16[16,64,128]{2,1,0:T(8,128)(2,1)} %get-tuple-element.97), calls=%async_computation | async-start | bytes 524288 | tf_op jit(solution)/shard_map/all_to_all | solution.py:543
  90.5 18.3 %all-to-all-done = bf16[16,64,128]{2,1,0:T(8,128)(2,1)S(1)} async-done(((bf16[16,64,128]{2,1,0:T(8,128)(2,1)}), bf16[16,64,128]{2,1,0:T(8,128)(2,1)S(1)}, u32[]{:S(2)}, u32[]{:S(2)}) %all-to-all-start) | async-done | bytes 262176 | tf_op jit(solution)/shard_map/all_to_all | solution.py:543
  109.4 4.0 %shard_map.231 = (f32[128,1024]{1,0:T(8,128)}, bf16[128,1024]{1,0:T(8,128)(2,1)}, bf16[1024,1024]{1,0:T(8,128)(2,1)}, bf16[4,32,1024]{2,1,0:T(8,128)(2,1)}) custom-call(s32[5]{0:T(128)} %stack.35.coords, bf16[1024,128]{1,0:T(8,128)(2,1)} %bitcast.102, bf16[128,1024]{1,0:T(8,128)(2,1)} %bitcast.95, f32[1,1024]{1,0:T(1,128)} %bitcast.107, ...), custom_call_target="tpu_custom_call" | custom-call | flops 4600000000 | bytes 1048576 | tf_op jit(solution)/shard_map/pallas_call | solution.py:64
  114.5 2.4 collective-permute-start.16
  119.1 3.8 %collective-permute-done.14 = bf16[128,1024]{1,0:T(8,128)(2,1)S(1)} collective-permute-done((bf16[128,1024]{1,0:T(8,128)(2,1)}, bf16[128,1024]{1,0:T(8,128)(2,1)S(1)}, u32[]{:S(2)}, u32[]{:S(2)}) %collective-permute-start.14) | collective-permute-done | bytes 262176 | tf_op jit(solution)/shard_map/ppermute | solution.py:45
  122.9 3.5 %collective-permute-done.16 = bf16[128,1024]{1,0:T(8,128)(2,1)S(1)} collective-permute-done((bf16[128,1024]{1,0:T(8,128)(2,1)}, bf16[128,1024]{1,0:T(8,128)(2,1)S(1)}, u32[]{:S(2)}, u32[]{:S(2)}) %collective-permute-start.16) | collective-permute-done | bytes 262176 | tf_op jit(solution)/shard_map/ppermute | solution.py:45
  126.5 2.5 fusion.9
  137.5 2.7 %collective-permute-start.19 = (bf16[128,1024]{1,0:T(8,128)(2,1)S(1)}, bf16[128,1024]{1,0:T(8,128)(2,1)S(1)}, u32[]{:S(2)}, u32[]{:S(2)}) collective-permute-start(bf16[128,1024]{1,0:T(8,128)(2,1)S(1)} %get-tuple-element.179), channel_id=1, source_target_pairs={{0,17},{1,16},{16,1},{17,0},{2,19},{3,18},{18,3},{19,2},{4,21},{5,... | collective-permute-start | bytes 786440 | tf_op jit(solution)/shard_map/ppermute | solution.py:45
  141.1 2.2 pad_maximum_fusion
  143.3 2.6 convolution_convert_fusion.3
  151.3 12.6 %all_to_all.15.refs_0_ = bf16[16,64,128]{2,1,0:T(8,128)(2,1)} all-to-all(bf16[16,64,128]{2,1,0:T(8,128)(2,1)S(1)} %bitcast.94), channel_id=1, replica_groups=mesh['x'=2,'c'=2,'z'=4,'y'=2,'r'=1] {'x','y','z'}, dimensions={0} | all-to-all | bytes 524288 | tf_op jit(solution)/shard_map/all_to_all | solution.py:587
  167.6 2.2 collective-permute-start.22
  169.7 20.7 %shard_map.232 = (f32[2048,128]{1,0:T(8,128)}, bf16[2048,128]{1,0:T(8,128)(2,1)}, bf16[16,64,128]{2,1,0:T(8,128)(2,1)}, f32[8,256]{1,0:T(8,128)}, f32[8,256]{1,0:T(8,128)}) custom-call(s32[5]{0:T(128)} %stack.35.coords, s32[16]{0:T(128)} %convert_reduce_fusion.cuts, f32[8,256]{1,0:T(8,128)} %pad.4.hvec, bf16[16,64,128]{2,1,0:T(8,128)(2,1)} %all_to_all.15.refs_0_, ...), custom_call_target="tpu_custom_call" | custom-call | flops 23000000512 | bytes 1048576 | tf_op jit(solution)/shard_map/pallas_call | solution.py:64
  196.9 2.1 collective-permute-start.26
  204.0 4.6 %collective-permute-done.26.refs_3_ = bf16[768,128]{1,0:T(8,128)(2,1)} collective-permute-done((bf16[768,128]{1,0:T(8,128)(2,1)}, bf16[768,128]{1,0:T(8,128)(2,1)}, u32[]{:S(2)}, u32[]{:S(2)}) %collective-permute-start.26) | collective-permute-done | bytes 196640 | tf_op jit(solution)/shard_map/ppermute | solution.py:45
  208.6 4.3 %shard_map.233 = (bf16[4,128,1024]{2,1,0:T(8,128)(2,1)}, f32[8,1024]{1,0:T(8,128)}, bf16[512,512]{1,0:T(8,128)(2,1)}, bf16[256,512]{1,0:T(8,128)(2,1)}) custom-call(s32[5]{0:T(128)} %stack.35.coords, bf16[768,128]{1,0:T(8,128)(2,1)} %get-tuple-element.132.refs_0_, bf16[768,128]{1,0:T(8,128)(2,1)} %collective-permute-done.24.refs_1_, ...), custom_call_target="tpu_custom_call" | custom-call | flops 4600000000 | bytes 1048576 | tf_op jit(solution)/shard_map/pallas_call | solution.py:64
  212.9 3.6 %all-to-all-start.2 = ((bf16[4,128,1024]{2,1,0:T(8,128)(2,1)}), bf16[4,128,1024]{2,1,0:T(8,128)(2,1)S(1)}, u32[]{:S(2)}, u32[]{:S(2)}) async-start(bf16[4,128,1024]{2,1,0:T(8,128)(2,1)} %get-tuple-element.138), calls=%async_computation.2 | async-start | bytes 2097152 | tf_op jit(solution)/shard_map/all_to_all | solution.py:658
  216.7 3.9 %shard_map.234 = (bf16[4,32,3072]{2,1,0:T(8,128)(2,1)}, bf16[4,32,3072]{2,1,0:T(8,128)(2,1)}) custom-call(s32[5]{0:T(128)} %stack.35.coords, bf16[512,512]{1,0:T(8,128)(2,1)} %get-tuple-element.141.pairs_t, bf16[256,512]{1,0:T(8,128)(2,1)} %get-tuple-element.142.queries_t, bf16[512,1024]{1,0:T(8,128)(2,1)} %get-tuple-element.136.refs_4_.rows_all), custom_call_target="tpu_custom_call" | custom-call | flops 4600000000 | bytes 1048576 | tf_op jit(solution)/shard_map/pallas_call | solution.py:64
  232.5 11.9 %all-to-all-done.2.refs_0_ = bf16[4,128,1024]{2,1,0:T(8,128)(2,1)S(1)} async-done(((bf16[4,128,1024]{2,1,0:T(8,128)(2,1)}), bf16[4,128,1024]{2,1,0:T(8,128)(2,1)S(1)}, u32[]{:S(2)}, u32[]{:S(2)}) %all-to-all-start.2) | async-done | bytes 1048608 | tf_op jit(solution)/shard_map/all_to_all | solution.py:658
  245.7 2.2 collective-permute-start.32
  249.5 2.6 shard_map.235
  256.2 2.0 collective-permute-done.35
  (276 shorter events, 84.0 us)
Async XLA Ops:
  7.2 101.5 %all-gather.6.cloned.1.call-start = ((), (), s32[]{:S(2)}) async-start(), calls=%async_computation.8 | async-start | bytes 2359296 | tf_op jit(solution)/shard_map/all_gather | solution.py:511
  9.6 26.6 %collective-permute-start = (bf16[128,1024]{1,0:T(8,128)(2,1)S(1)}, bf16[128,1024]{1,0:T(8,128)(2,1)S(1)}, u32[]{:S(2)}, u32[]{:S(2)}) collective-permute-start(bf16[128,1024]{1,0:T(8,128)(2,1)S(1)} %fusion.31.refs_0_), channel_id=1, source_target_pairs={{0,2},{2,0},{4,6},{6,4},{1,3},{3,1},{5,7},{7,5},{8,10},{10,8},{12,... | collective-permute-start | bytes 786440 | tf_op jit(solution)/shard_map/ppermute | solution.py:45
  12.7 23.5 %collective-permute-start.1 = (bf16[128,1024]{1,0:T(8,128)(2,1)S(1)}, bf16[128,1024]{1,0:T(8,128)(2,1)S(1)}, u32[]{:S(2)}, u32[]{:S(2)}) collective-permute-start(bf16[128,1024]{1,0:T(8,128)(2,1)S(1)} %fusion.31.refs_0_), channel_id=1, source_target_pairs={{0,4},{2,6},{4,0},{6,2},{1,5},{3,7},{5,1},{7,3},{8,12},{10,14},{12... | collective-permute-start | bytes 786440 | tf_op jit(solution)/shard_map/ppermute | solution.py:45
  15.3 20.9 %collective-permute-start.2 = (bf16[128,1024]{1,0:T(8,128)(2,1)S(1)}, bf16[128,1024]{1,0:T(8,128)(2,1)S(1)}, u32[]{:S(2)}, u32[]{:S(2)}) collective-permute-start(bf16[128,1024]{1,0:T(8,128)(2,1)S(1)} %fusion.31.refs_0_), channel_id=1, source_target_pairs={{0,6},{2,4},{4,2},{6,0},{1,7},{3,5},{5,3},{7,1},{8,14},{10,12},{12... | collective-permute-start | bytes 786440 | tf_op jit(solution)/shard_map/ppermute | solution.py:45
  18.7 10.1 %collective-permute-start.5 = (bf16[32,4096]{1,0:T(8,128)(2,1)S(1)}, bf16[32,4096]{1,0:T(8,128)(2,1)S(1)}, u32[]{:S(2)}, u32[]{:S(2)}) collective-permute-start(bf16[32,4096]{1,0:T(8,128)(2,1)S(1)} %constant_dynamic-update-slice_fusion.1.refs_4_), channel_id=1, source_target_pairs={{0,17},{1,16},{16,1},{17,0},{2,19},{3,18},{18,3},{19,2},{4,21},{5,... | collective-permute-start | bytes 786440 | tf_op jit(solution)/shard_map/ppermute | solution.py:45
  21.4 12.0 %collective-permute-start.4 = (bf16[32,4096]{1,0:T(8,128)(2,1)S(1)}, bf16[32,4096]{1,0:T(8,128)(2,1)S(1)}, u32[]{:S(2)}, u32[]{:S(2)}) collective-permute-start(bf16[32,4096]{1,0:T(8,128)(2,1)S(1)} %constant_dynamic-update-slice_fusion.1.refs_4_), channel_id=1, source_target_pairs={{0,16},{1,17},{16,0},{17,1},{2,18},{3,19},{18,2},{19,3},{4,20},{5,... | collective-permute-start | bytes 786440 | tf_op jit(solution)/shard_map/ppermute | solution.py:45
  36.3 90.1 %all-gather.4.cloned.1.call-start = ((), (), s32[]{:S(2)}) async-start(), calls=%async_computation.5 | async-start | bytes 4866048 | tf_op jit(solution)/shard_map/all_gather | solution.py:472
  44.8 8.9 %collective-permute-start.9 = (bf16[768,128]{1,0:T(8,128)(2,1)}, bf16[768,128]{1,0:T(8,128)(2,1)S(1)}, u32[]{:S(2)}, u32[]{:S(2)}) collective-permute-start(bf16[768,128]{1,0:T(8,128)(2,1)} %get-tuple-element.92), channel_id=1, source_target_pairs={{0,17},{1,16},{16,1},{17,0},{2,19},{3,18},{18,3},{19,2},{4,21},{5,... | collective-permute-start | bytes 589832 | tf_op jit(solution)/shard_map/ppermute | solution.py:45
  47.4 9.9 %collective-permute-start.8 = (bf16[768,128]{1,0:T(8,128)(2,1)}, bf16[768,128]{1,0:T(8,128)(2,1)S(1)}, u32[]{:S(2)}, u32[]{:S(2)}) collective-permute-start(bf16[768,128]{1,0:T(8,128)(2,1)} %get-tuple-element.91), channel_id=1, source_target_pairs={{0,16},{1,17},{16,0},{17,1},{2,18},{3,19},{18,2},{19,3},{4,20},{5,... | collective-permute-start | bytes 589832 | tf_op jit(solution)/shard_map/ppermute | solution.py:45
  47.9 9.4 %collective-permute-start.7 = (bf16[768,128]{1,0:T(8,128)(2,1)}, bf16[768,128]{1,0:T(8,128)(2,1)S(1)}, u32[]{:S(2)}, u32[]{:S(2)}) collective-permute-start(bf16[768,128]{1,0:T(8,128)(2,1)} %get-tuple-element.90), channel_id=1, source_target_pairs={{0,1},{1,0},{16,17},{17,16},{2,3},{3,2},{18,19},{19,18},{4,5},{5,4... | collective-permute-start | bytes 589832 | tf_op jit(solution)/shard_map/ppermute | solution.py:45
  60.2 23.1 %collective-permute-start.11 = (bf16[128,1024]{1,0:T(8,128)(2,1)S(1)}, bf16[128,1024]{1,0:T(8,128)(2,1)S(1)}, u32[]{:S(2)}, u32[]{:S(2)}) collective-permute-start(bf16[128,1024]{1,0:T(8,128)(2,1)S(1)} %bitcast.90), channel_id=1, source_target_pairs={{0,1},{1,0},{16,17},{17,16},{2,3},{3,2},{18,19},{19,18},{4,5},{5,4... | collective-permute-start | bytes 786440 | tf_op jit(solution)/shard_map/ppermute | solution.py:45
  61.6 21.8 %collective-permute-start.12 = (bf16[128,1024]{1,0:T(8,128)(2,1)S(1)}, bf16[128,1024]{1,0:T(8,128)(2,1)S(1)}, u32[]{:S(2)}, u32[]{:S(2)}) collective-permute-start(bf16[128,1024]{1,0:T(8,128)(2,1)S(1)} %bitcast.91), channel_id=1, source_target_pairs={{0,16},{1,17},{16,0},{17,1},{2,18},{3,19},{18,2},{19,3},{4,20},{5,... | collective-permute-start | bytes 786440 | tf_op jit(solution)/shard_map/ppermute | solution.py:45
  63.1 20.3 %collective-permute-start.13 = (bf16[128,1024]{1,0:T(8,128)(2,1)S(1)}, bf16[128,1024]{1,0:T(8,128)(2,1)S(1)}, u32[]{:S(2)}, u32[]{:S(2)}) collective-permute-start(bf16[128,1024]{1,0:T(8,128)(2,1)S(1)} %bitcast.92), channel_id=1, source_target_pairs={{0,17},{1,16},{16,1},{17,0},{2,19},{3,18},{18,3},{19,2},{4,21},{5,... | collective-permute-start | bytes 786440 | tf_op jit(solution)/shard_map/ppermute | solution.py:45
  83.3 25.4 %all-to-all-start = ((bf16[16,64,128]{2,1,0:T(8,128)(2,1)}), bf16[16,64,128]{2,1,0:T(8,128)(2,1)S(1)}, u32[]{:S(2)}, u32[]{:S(2)}) async-start(bf16[16,64,128]{2,1,0:T(8,128)(2,1)} %get-tuple-element.97), calls=%async_computation | async-start | bytes 524288 | tf_op jit(solution)/shard_map/all_to_all | solution.py:543
  90.1 130.4 %reduce-scatter.3.cloned.1.call-start = ((), (), s32[]{:S(2)}) async-start(), calls=%async_computation.6 | async-start | bytes 4866048 | tf_op jit(solution)/shard_map/reduce_scatter | solution.py:597
  113.4 9.4 %collective-permute-start.14 = (bf16[128,1024]{1,0:T(8,128)(2,1)}, bf16[128,1024]{1,0:T(8,128)(2,1)S(1)}, u32[]{:S(2)}, u32[]{:S(2)}) collective-permute-start(bf16[128,1024]{1,0:T(8,128)(2,1)} %get-tuple-element.104), channel_id=1, source_target_pairs={{0,1},{1,0},{16,17},{17,16},{2,3},{3,2},{18,19},{19,18},{4,5},{5,4... | collective-permute-start | bytes 786440 | tf_op jit(solution)/shard_map/ppermute | solution.py:45
  113.4 9.4 %collective-permute-start.15 = (bf16[128,1024]{1,0:T(8,128)(2,1)}, bf16[128,1024]{1,0:T(8,128)(2,1)S(1)}, u32[]{:S(2)}, u32[]{:S(2)}) collective-permute-start(bf16[128,1024]{1,0:T(8,128)(2,1)} %get-tuple-element.104), channel_id=1, source_target_pairs={{0,16},{1,17},{16,0},{17,1},{2,18},{3,19},{18,2},{19,3},{4,20},{5,... | collective-permute-start | bytes 786440 | tf_op jit(solution)/shard_map/ppermute | solution.py:45
  114.5 11.9 %collective-permute-start.16 = (bf16[128,1024]{1,0:T(8,128)(2,1)}, bf16[128,1024]{1,0:T(8,128)(2,1)S(1)}, u32[]{:S(2)}, u32[]{:S(2)}) collective-permute-start(bf16[128,1024]{1,0:T(8,128)(2,1)} %get-tuple-element.104), channel_id=1, source_target_pairs={{0,17},{1,16},{16,1},{17,0},{2,19},{3,18},{18,3},{19,2},{4,21},{5,... | collective-permute-start | bytes 786440 | tf_op jit(solution)/shard_map/ppermute | solution.py:45
  136.7 9.3 %collective-permute-start.17 = (bf16[128,1024]{1,0:T(8,128)(2,1)}, bf16[128,1024]{1,0:T(8,128)(2,1)S(1)}, u32[]{:S(2)}, u32[]{:S(2)}) collective-permute-start(bf16[128,1024]{1,0:T(8,128)(2,1)} %get-tuple-element.181), channel_id=1, source_target_pairs={{0,1},{1,0},{16,17},{17,16},{2,3},{3,2},{18,19},{19,18},{4,5},{5,4... | collective-permute-start | bytes 786440 | tf_op jit(solution)/shard_map/ppermute | solution.py:45
  137.0 9.0 %collective-permute-start.18 = (bf16[128,1024]{1,0:T(8,128)(2,1)S(1)}, bf16[128,1024]{1,0:T(8,128)(2,1)S(1)}, u32[]{:S(2)}, u32[]{:S(2)}) collective-permute-start(bf16[128,1024]{1,0:T(8,128)(2,1)S(1)} %get-tuple-element.180), channel_id=1, source_target_pairs={{0,16},{1,17},{16,0},{17,1},{2,18},{3,19},{18,2},{19,3},{4,20},{5,... | collective-permute-start | bytes 786440 | tf_op jit(solution)/shard_map/ppermute | solution.py:45
  137.5 10.5 %collective-permute-start.19 = (bf16[128,1024]{1,0:T(8,128)(2,1)S(1)}, bf16[128,1024]{1,0:T(8,128)(2,1)S(1)}, u32[]{:S(2)}, u32[]{:S(2)}) collective-permute-start(bf16[128,1024]{1,0:T(8,128)(2,1)S(1)} %get-tuple-element.179), channel_id=1, source_target_pairs={{0,17},{1,16},{16,1},{17,0},{2,19},{3,18},{18,3},{19,2},{4,21},{5,... | collective-permute-start | bytes 786440 | tf_op jit(solution)/shard_map/ppermute | solution.py:45
  166.3 25.7 %collective-permute-start.20 = (bf16[288,1024]{1,0:T(8,128)(2,1)}, bf16[288,1024]{1,0:T(8,128)(2,1)S(1)}, u32[]{:S(2)}, u32[]{:S(2)}) collective-permute-start(bf16[288,1024]{1,0:T(8,128)(2,1)} %get-tuple-element.205), channel_id=1, source_target_pairs={{0,1},{1,0},{16,17},{17,16},{2,3},{3,2},{18,19},{19,18},{4,5},{5,4... | collective-permute-start | bytes 1769480 | tf_op jit(solution)/shard_map/ppermute | solution.py:45
  166.7 25.3 %collective-permute-start.21 = (bf16[288,1024]{1,0:T(8,128)(2,1)}, bf16[288,1024]{1,0:T(8,128)(2,1)S(1)}, u32[]{:S(2)}, u32[]{:S(2)}) collective-permute-start(bf16[288,1024]{1,0:T(8,128)(2,1)} %get-tuple-element.206), channel_id=1, source_target_pairs={{0,16},{1,17},{16,0},{17,1},{2,18},{3,19},{18,2},{19,3},{4,20},{5,... | collective-permute-start | bytes 1769480 | tf_op jit(solution)/shard_map/ppermute | solution.py:45
  167.6 24.4 %collective-permute-start.22 = (bf16[288,1024]{1,0:T(8,128)(2,1)}, bf16[288,1024]{1,0:T(8,128)(2,1)S(1)}, u32[]{:S(2)}, u32[]{:S(2)}) collective-permute-start(bf16[288,1024]{1,0:T(8,128)(2,1)} %get-tuple-element.204), channel_id=1, source_target_pairs={{0,17},{1,16},{16,1},{17,0},{2,19},{3,18},{18,3},{19,2},{4,21},{5,... | collective-permute-start | bytes 1769480 | tf_op jit(solution)/shard_map/ppermute | solution.py:45
  195.9 8.1 %collective-permute-start.25 = (bf16[768,128]{1,0:T(8,128)(2,1)}, bf16[768,128]{1,0:T(8,128)(2,1)}, u32[]{:S(2)}, u32[]{:S(2)}) collective-permute-start(bf16[768,128]{1,0:T(8,128)(2,1)} %get-tuple-element.134), channel_id=1, source_target_pairs={{0,16},{1,17},{16,0},{17,1},{2,18},{3,19},{18,2},{19,3},{4,20},{5,... | collective-permute-start | bytes 589832 | tf_op jit(solution)/shard_map/ppermute | solution.py:45
  196.9 11.6 %collective-permute-start.26 = (bf16[768,128]{1,0:T(8,128)(2,1)}, bf16[768,128]{1,0:T(8,128)(2,1)}, u32[]{:S(2)}, u32[]{:S(2)}) collective-permute-start(bf16[768,128]{1,0:T(8,128)(2,1)} %get-tuple-element.135), channel_id=1, source_target_pairs={{0,17},{1,16},{16,1},{17,0},{2,19},{3,18},{18,3},{19,2},{4,21},{5,... | collective-permute-start | bytes 589832 | tf_op jit(solution)/shard_map/ppermute | solution.py:45
  212.9 31.5 %all-to-all-start.2 = ((bf16[4,128,1024]{2,1,0:T(8,128)(2,1)}), bf16[4,128,1024]{2,1,0:T(8,128)(2,1)S(1)}, u32[]{:S(2)}, u32[]{:S(2)}) async-start(bf16[4,128,1024]{2,1,0:T(8,128)(2,1)} %get-tuple-element.138), calls=%async_computation.2 | async-start | bytes 2097152 | tf_op jit(solution)/shard_map/all_to_all | solution.py:658
  216.5 42.5 %reduce-scatter.5.cloned.1.call-start = ((), (), s32[]{:S(2)}) async-start(), calls=%async_computation.7 | async-start | bytes 589824 | tf_op jit(solution)/shard_map/reduce_scatter | solution.py:673
  220.5 10.6 %collective-permute-start.27 = (bf16[4,32,3072]{2,1,0:T(8,128)(2,1)}, bf16[4,32,3072]{2,1,0:T(8,128)(2,1)}, u32[]{:S(2)}, u32[]{:S(2)}) collective-permute-start(bf16[4,32,3072]{2,1,0:T(8,128)(2,1)} %get-tuple-element.147), channel_id=1, source_target_pairs={{0,8},{8,0},{1,9},{9,1},{2,10},{10,2},{3,11},{11,3},{4,12},{12,4},... | collective-permute-start | bytes 2359304 | tf_op jit(solution)/shard_map/ppermute | solution.py:45
  244.4 9.6 %collective-permute-start.34 = (f32[2560]{0:T(1024)S(1)}, f32[2560]{0:T(1024)S(1)}, u32[]{:S(2)}, u32[]{:S(2)}) collective-permute-start(f32[2560]{0:T(1024)S(1)} %add_add_fusion.1), channel_id=1, source_target_pairs={{0,6},{2,4},{4,2},{6,0},{1,7},{3,5},{5,3},{7,1},{8,14},{10,12},{12... | collective-permute-start | bytes 30728 | tf_op jit(solution)/shard_map/ppermute | solution.py:45
  245.7 8.3 %collective-permute-start.32 = (f32[2560]{0:T(1024)S(1)}, f32[2560]{0:T(1024)S(1)}, u32[]{:S(2)}, u32[]{:S(2)}) collective-permute-start(f32[2560]{0:T(1024)S(1)} %add_add_fusion.1), channel_id=1, source_target_pairs={{0,2},{2,0},{4,6},{6,4},{1,3},{3,1},{5,7},{7,5},{8,10},{10,8},{12,... | collective-permute-start | bytes 30728 | tf_op jit(solution)/shard_map/ppermute | solution.py:45
  248.0 8.2 %collective-permute-start.36 = (bf16[32,3072]{1,0:T(8,128)(2,1)S(1)}, bf16[32,3072]{1,0:T(8,128)(2,1)S(1)}, u32[]{:S(2)}, u32[]{:S(2)}) collective-permute-start(bf16[32,3072]{1,0:T(8,128)(2,1)S(1)} %get-tuple-element.185), channel_id=1, source_target_pairs={{0,16},{1,17},{16,0},{17,1},{2,18},{3,19},{18,2},{19,3},{4,20},{5,... | collective-permute-start | bytes 589832 | tf_op jit(solution)/shard_map/ppermute | solution.py:45
  (59 other events, 445.3 us)
Sparse Core Ops, SparseCore 0:
  36.4 30.4 all-gather.5
  68.5 53.2 all-gather.3
  164.0 48.8 reduce-scatter.2
  225.6 31.3 reduce-scatter.4
